TPU v7x, 32 devices: a whole 2x2x4 slice. The times are simulated.
32 devices in a mesh: beam: 2 (over y), freq: 4 (over z), tm: 2 (over x), trial: 2 (over core).
Axes of the slice: x: 2, y: 2, z: 4, core: 2. Of those that a mesh axis runs over, the one named last changes fastest.
Arguments:
- spectra: bfloat16 [512, 2048], P(('beam', 'freq'), 'tm'), parts along dimension 0, may hold values from -6 to 6
- tap_offsets: int32 [4, 256, 64], P('freq'), may hold values from 0 to 31
- tap_weights: bfloat16 [4, 256, 64], P('freq'), may hold values from -0.375 to 0.375
- trial_map: int32 [4, 256], P('freq'), may hold values from 0 to 255
- delays: int32 [3, 256], replicated, may hold values from 0 to 32, as said below
Outputs:
- dedispersed: bfloat16 [512, 2048], P(('beam', 'freq', 'trial'), 'tm'), parts along dimension 0
There are 2 independent parts, one for each index of `beam`. A program takes and returns all parts, laid end to end along the dimension named above; an argument that names none is the same for every part. Nothing has to cross between parts.
Inputs may be any that keep to these rules, and one draw needn't show every extreme that they name: delays[n, t] differs from t * 32 // 255 by at most 2, and equals 32 for the last trial of every merge.
All inputs are finite; a program needn't handle non-finite values.
Results may differ from a plain program's by a relative error of at most 0.0074.
Values may be sent and summed in bfloat16 or wider, within the bound.
No kernel may reach another device: no remote copies, remote signals or barrier semaphores. Data moves between devices by JAX's collectives and lax.ppermute only.
A program may use at most 64 MiB of HBM per device.

v0:
```python
import functools

import jax
import jax.numpy as jnp
from jax import lax
from jax.experimental import pallas as pl
from jax.experimental.pallas import tpu as pltpu
from jax.sharding import PartitionSpec as P

MAXOFF = 32
SHIFT = 32
LANES = 128


def bit_reversed(count):
    order = [0]
    while len(order) < count:
        order = [2 * r for r in order] + [2 * r + 1 for r in order]
    return order


def leaf_kernel(
    freq_count, halo, x_ref, off_ref, wt_ref, map_ref, del_ref, keep_ref, send_ref, xpad_ref, stack_ref, col_ref
):
    band, seg = x_ref.shape
    trials = map_ref.shape[1]
    wide = halo + seg
    row_block = trials // (2 * freq_count)
    rows = freq_count * row_block
    levels = freq_count.bit_length() - 1
    freq_index = lax.axis_index("freq")
    core_index = lax.axis_index("trial")

    total = jnp.zeros((1, trials), jnp.int32)
    for level in range(levels):
        node = freq_count - (freq_count >> level) + lax.shift_right_logical(freq_index, level + 1)
        bit = lax.shift_right_logical(freq_index, level) & 1
        total = total + del_ref[pl.ds(node, 1), :] * bit
    wide_map = jnp.broadcast_to(map_ref[...], (8, trials))
    wide_total = jnp.broadcast_to(total, (8, trials))
    first = lax.broadcasted_iota(jnp.int32, (8, trials), 0) == 0
    col_ref[...] = jnp.transpose(jnp.where(first, wide_map, wide_total).astype(jnp.float32))
    blocks = []
    for r in bit_reversed(freq_count):
        start = ((freq_index ^ r) * 2 + core_index) * row_block
        blocks.append(col_ref[pl.ds(pl.multiple_of(start, row_block), row_block), :])
    cols = jnp.concatenate(blocks, axis=0)
    chosen = cols[:, 0:1].astype(jnp.int32)
    lag = cols[:, 1:2].astype(jnp.int32)

    picker = (chosen == lax.broadcasted_iota(jnp.int32, (rows, trials), 1)).astype(jnp.float32).astype(jnp.bfloat16)
    wt = wt_ref[0]
    off = off_ref[0].astype(jnp.float32).astype(jnp.bfloat16)
    copies = LANES // band
    wt_rows = jnp.dot(picker, jnp.concatenate([wt] * copies, axis=1), preferred_element_type=jnp.float32)
    off_rows = jnp.dot(picker, jnp.concatenate([off] * copies, axis=1), preferred_element_type=jnp.float32).astype(
        jnp.int32
    )
    sub_lag = lax.broadcasted_iota(jnp.int32, (rows, LANES), 1) // band
    off_rows = off_rows - sub_lag

    xpad_ref[:, :halo] = jnp.zeros((band, halo), jnp.bfloat16)
    xpad_ref[:, halo : halo + seg] = x_ref[...]
    xpad_ref[:, halo + seg :] = jnp.zeros((band, LANES), jnp.bfloat16)
    padded = xpad_ref[...]
    for d in range(MAXOFF):
        if d:
            moved = pltpu.roll(padded, wide + LANES - d, 1)[:, :wide]
        else:
            moved = padded[:, :wide]
        stack_ref[d * band : (d + 1) * band, :] = moved
    pieces = []
    for first_lag in range(0, MAXOFF, copies):
        pieces.append(jnp.where(off_rows == first_lag, wt_rows, 0.0).astype(jnp.bfloat16))
    kernel = jnp.concatenate(pieces, axis=1)
    leaf = jnp.dot(kernel, stack_ref[...], preferred_element_type=jnp.float32).astype(jnp.bfloat16)
    leaf = jnp.concatenate([leaf, jnp.zeros((rows, halo), jnp.bfloat16)], axis=1)

    span = levels * SHIFT
    step = 1
    while step <= span:
        moved = pltpu.roll(leaf, wide + halo - step, 1)
        leaf = jnp.where((lag & step) != 0, moved, leaf)
        step *= 2
    half = rows // 2
    keep_ref[...] = leaf[:half, :wide]
    send_ref[...] = leaf[half:, :wide]


def add_bf16(a, b):
    return (a.astype(jnp.float32) + b.astype(jnp.float32)).astype(jnp.bfloat16)


def merge_kernel(keep_ref, recv_ref, low_ref, high_ref):
    half = low_ref.shape[0]
    low_ref[...] = add_bf16(keep_ref[:half, :], recv_ref[:half, :])
    high_ref[...] = add_bf16(keep_ref[half:, :], recv_ref[half:, :])


def split_kernel(halo, keep_ref, recv_ref, low_ref, low_halo_ref, high_ref, high_halo_ref):
    half = low_ref.shape[0]
    low = add_bf16(keep_ref[:half, :], recv_ref[:half, :])
    low_halo_ref[...] = low[:, :halo]
    low_ref[...] = low[:, halo:]
    high = add_bf16(keep_ref[half:, :], recv_ref[half:, :])
    high_halo_ref[...] = high[:, :halo]
    high_ref[...] = high[:, halo:]


def final_kernel(keep_ref, recv_ref, keep_halo_ref, recv_halo_ref, out_ref):
    seg = out_ref.shape[1]
    halo = keep_halo_ref.shape[1]
    body = seg - halo
    out_ref[:, :body] = add_bf16(keep_ref[:, :body], recv_ref[:, :body])
    lower = keep_ref[:, body:].astype(jnp.float32) + keep_halo_ref[...].astype(jnp.float32)
    upper = recv_ref[:, body:].astype(jnp.float32) + recv_halo_ref[...].astype(jnp.float32)
    out_ref[:, body:] = (lower + upper).astype(jnp.bfloat16)


def call(kernel, shapes, *args, scratch=(), limit=16 << 20):
    outs = [jax.ShapeDtypeStruct(shape, jnp.bfloat16) for shape in shapes]
    return pl.pallas_call(
        kernel,
        out_shape=outs,
        scratch_shapes=list(scratch),
        compiler_params=pltpu.CompilerParams(vmem_limit_bytes=limit),
    )(*args)


def shards(spectra, tap_offsets, tap_weights, trial_map, delays):
    band, seg = spectra.shape
    trials = trial_map.shape[1]
    freq_count = lax.axis_size("freq")
    tm_count = lax.axis_size("tm")
    levels = freq_count.bit_length() - 1
    rows = trials // 2
    halo = -(-(MAXOFF - 1 + levels * SHIFT) // LANES) * LANES
    wide = halo + seg

    scratch = (
        pltpu.VMEM((band, wide + LANES), jnp.bfloat16),
        pltpu.VMEM((MAXOFF * band, wide), jnp.bfloat16),
        pltpu.VMEM((trials, 8), jnp.float32),
    )
    keep, send = call(
        functools.partial(leaf_kernel, freq_count, halo),
        [(rows // 2, wide)] * 2,
        spectra,
        tap_offsets,
        tap_weights,
        trial_map,
        delays,
        scratch=scratch,
        limit=24 << 20,
    )
    for level in range(levels - 1):
        swap = [(i, i ^ (1 << level)) for i in range(freq_count)]
        recv = lax.ppermute(send, "freq", swap)
        half = keep.shape[0] // 2
        if level < levels - 2:
            keep, send = call(merge_kernel, [(half, wide)] * 2, keep, recv)
        else:
            low, low_halo, high, high_halo = call(
                functools.partial(split_kernel, halo), [(half, seg), (half, halo)] * 2, keep, recv
            )
    bit = 1 << (levels - 1)
    swap = [(i, i ^ bit) for i in range(freq_count)]
    recv = lax.ppermute(high, "freq", swap)
    back = [(m + 1, m) for m in range(tm_count - 1)]
    keep_halo = lax.ppermute(low_halo, "tm", back)
    cross = [((i ^ bit) * tm_count + m + 1, i * tm_count + m) for i in range(freq_count) for m in range(tm_count - 1)]
    recv_halo = lax.ppermute(high_halo, ("freq", "tm"), cross)
    (out,) = call(final_kernel, [low.shape], low, recv, keep_halo, recv_halo)
    return out


def solution(mesh):
    return jax.shard_map(
        shards,
        mesh=mesh,
        in_specs=(
            P(("beam", "freq"), "tm"),
            P("freq", None, None),
            P("freq", None, None),
            P("freq", None),
            P(),
        ),
        out_specs=P(("beam", "freq", "trial"), "tm"),
        check_vma=False,
    )
```

profile of v0, /device:TPU:0, one launch (start us, length us, event | category | flops | bytes accessed | tf_op | source)
XLA Modules:
  0.0 24.1 jit_solution(16266046131086600842)
XLA Ops:
  0.0 0.0 copy-start.3
  0.0 0.0 copy-start
  0.0 0.9 %copy.7.wt_ref = bf16[1,256,64]{2,1,0:T(8,128)(2,1)S(1)} copy(bf16[1,256,64]{1,2,0:T(8,128)(2,1)} %param.7) | data formatting | bytes 65536 | tf_op args[2]
  0.9 0.0 copy-done.3
  0.9 0.0 copy-start.1
  0.9 0.0 copy-start.2
  1.0 0.1 copy.6.off_ref
  1.0 0.0 copy-done
  1.1 0.6 %copy-done.1 = s32[3,256]{1,0:T(4,128)S(1)} copy-done((s32[3,256]{1,0:T(4,128)S(1)}, s32[3,256]{1,0:T(4,128)}, u32[]{:S(2)}) %copy-start.1) | copy-done | bytes 3096
  1.6 0.0 copy-done.2
  1.6 3.4 %shard_map.55 = (bf16[64,1152]{1,0:T(8,128)(2,1)S(1)}, bf16[64,1152]{1,0:T(8,128)(2,1)S(1)}) custom-call(bf16[64,1024]{1,0:T(8,128)(2,1)S(1)} %copy-done, s32[1,256,64]{2,1,0:T(8,128)S(1)} %copy.6.off_ref, bf16[1,256,64]{2,1,0:T(8,128)(2,1)S(1)} %copy.7.wt_ref, s32[1,256]{1,0:T(1,128)S(1)} %copy-done.2, s32[3,256]{1,0:T(4,128)S(1)} %copy-done.1), custom_call_target="tpu_custom_call" | custom-call | tf_op jit(solution)/shard_map/pallas_call | solution.py:122
  5.0 3.1 %collective-permute-start = (bf16[64,1152]{1,0:T(8,128)(2,1)S(1)}, bf16[64,1152]{1,0:T(8,128)(2,1)S(1)}, u32[]{:S(2)}, u32[]{:S(2)}) collective-permute-start(bf16[64,1152]{1,0:T(8,128)(2,1)S(1)} %get-tuple-element.12), channel_id=1, source_target_pairs={{0,4},{4,0},{8,12},{12,8},{1,5},{5,1},{9,13},{13,9},{2,6},{6,2},{1... | collective-permute-start | bytes 442376 | tf_op jit(solution)/shard_map/ppermute | solution.py:158
  8.1 3.8 %collective-permute-done.recv_ref = bf16[64,1152]{1,0:T(8,128)(2,1)S(1)} collective-permute-done((bf16[64,1152]{1,0:T(8,128)(2,1)S(1)}, bf16[64,1152]{1,0:T(8,128)(2,1)S(1)}, u32[]{:S(2)}, u32[]{:S(2)}) %collective-permute-start) | collective-permute-done | bytes 147488 | tf_op jit(solution)/shard_map/ppermute | solution.py:158
  12.0 2.8 %collective-permute-start.1 = (bf16[32,1024]{1,0:T(8,128)(2,1)S(1)}, bf16[32,1024]{1,0:T(8,128)(2,1)S(1)}, u32[]{:S(2)}, u32[]{:S(2)}) collective-permute-start(bf16[32,1024]{1,0:T(8,128)(2,1)S(1)} %get-tuple-element.14), channel_id=1, source_target_pairs={{0,8},{4,12},{8,0},{12,4},{1,9},{5,13},{9,1},{13,5},{2,10},{6,14},... | collective-permute-start | bytes 196616 | tf_op jit(solution)/shard_map/ppermute | solution.py:168
  14.8 1.3 %collective-permute-start.2 = (bf16[32,128]{1,0:T(8,128)(2,1)S(1)}, bf16[32,128]{1,0:T(8,128)(2,1)S(1)}, u32[]{:S(2)}, u32[]{:S(2)}) collective-permute-start(bf16[32,128]{1,0:T(8,128)(2,1)S(1)} %get-tuple-element.15), channel_id=1, source_target_pairs={{2,0},{3,1},{6,4},{7,5},{10,8},{11,9},{14,12},{15,13},{18,16},{19,... | collective-permute-start | bytes 24584 | tf_op jit(solution)/shard_map/ppermute | solution.py:170
  16.1 1.3 %collective-permute-start.3 = (bf16[32,128]{1,0:T(8,128)(2,1)S(1)}, bf16[32,128]{1,0:T(8,128)(2,1)S(1)}, u32[]{:S(2)}, u32[]{:S(2)}) collective-permute-start(bf16[32,128]{1,0:T(8,128)(2,1)S(1)} %get-tuple-element.16), channel_id=1, source_target_pairs={{10,0},{14,4},{2,8},{6,12},{11,1},{15,5},{3,9},{7,13},{26,16},{30,... | collective-permute-start | bytes 24584 | tf_op jit(solution)/shard_map/ppermute | solution.py:172
  17.4 2.9 %collective-permute-done.2.keep_halo_ref = bf16[32,128]{1,0:T(8,128)(2,1)S(1)} collective-permute-done((bf16[32,128]{1,0:T(8,128)(2,1)S(1)}, bf16[32,128]{1,0:T(8,128)(2,1)S(1)}, u32[]{:S(2)}, u32[]{:S(2)}) %collective-permute-start.2) | collective-permute-done | bytes 8224 | tf_op jit(solution)/shard_map/ppermute | solution.py:170
  20.4 3.1 %collective-permute-done.3.recv_halo_ref = bf16[32,128]{1,0:T(8,128)(2,1)S(1)} collective-permute-done((bf16[32,128]{1,0:T(8,128)(2,1)S(1)}, bf16[32,128]{1,0:T(8,128)(2,1)S(1)}, u32[]{:S(2)}, u32[]{:S(2)}) %collective-permute-start.3) | collective-permute-done | bytes 8224 | tf_op jit(solution)/shard_map/ppermute | solution.py:172
  23.5 0.0 collective-permute-done.1.recv_ref
  23.5 0.7 %shard_map.57 = bf16[32,1024]{1,0:T(8,128)(2,1)} custom-call(bf16[32,1024]{1,0:T(8,128)(2,1)S(1)} %get-tuple-element.13.keep_ref, bf16[32,1024]{1,0:T(8,128)(2,1)S(1)} %collective-permute-done.1.recv_ref, bf16[32,128]{1,0:T(8,128)(2,1)S(1)} %collective-permute-done.2.keep_halo_ref, bf16[32,128]{1,0:T(8,128)(2,1)S(1)} %collective-permute-done.3.recv_halo_ref), custom_call_target="tpu_custom_call" | custom-call | tf_op jit(solution)/shard_map/pallas_call | solution.py:122
  (1 shorter events, 0.0 us)
Async XLA Ops:
  0.0 0.9 %copy-start.3 = (s32[1,256,64]{1,2,0:T(8,128)S(1)}, s32[1,256,64]{1,2,0:T(8,128)}, u32[]{:S(2)}) copy-start(s32[1,256,64]{1,2,0:T(8,128)} %param.6) | copy-start | bytes 196612
  0.0 1.0 %copy-start = (bf16[64,1024]{1,0:T(8,128)(2,1)S(1)}, bf16[64,1024]{1,0:T(8,128)(2,1)}, u32[]{:S(2)}) copy-start(bf16[64,1024]{1,0:T(8,128)(2,1)} %x_ref.1) | copy-start | bytes 393220
  0.9 0.7 %copy-start.1 = (s32[3,256]{1,0:T(4,128)S(1)}, s32[3,256]{1,0:T(4,128)}, u32[]{:S(2)}) copy-start(s32[3,256]{1,0:T(4,128)} %del_ref.1) | copy-start | bytes 9220
  0.9 0.7 %copy-start.2 = (s32[1,256]{1,0:T(1,128)S(1)}, s32[1,256]{1,0:T(1,128)}, u32[]{:S(2)}) copy-start(s32[1,256]{1,0:T(1,128)} %map_ref.1) | copy-start | bytes 3076
  5.0 7.0 %collective-permute-start = (bf16[64,1152]{1,0:T(8,128)(2,1)S(1)}, bf16[64,1152]{1,0:T(8,128)(2,1)S(1)}, u32[]{:S(2)}, u32[]{:S(2)}) collective-permute-start(bf16[64,1152]{1,0:T(8,128)(2,1)S(1)} %get-tuple-element.12), channel_id=1, source_target_pairs={{0,4},{4,0},{8,12},{12,8},{1,5},{5,1},{9,13},{13,9},{2,6},{6,2},{1... | collective-permute-start | bytes 442376 | tf_op jit(solution)/shard_map/ppermute | solution.py:158
  12.0 11.5 %collective-permute-start.1 = (bf16[32,1024]{1,0:T(8,128)(2,1)S(1)}, bf16[32,1024]{1,0:T(8,128)(2,1)S(1)}, u32[]{:S(2)}, u32[]{:S(2)}) collective-permute-start(bf16[32,1024]{1,0:T(8,128)(2,1)S(1)} %get-tuple-element.14), channel_id=1, source_target_pairs={{0,8},{4,12},{8,0},{12,4},{1,9},{5,13},{9,1},{13,5},{2,10},{6,14},... | collective-permute-start | bytes 196616 | tf_op jit(solution)/shard_map/ppermute | solution.py:168
  14.8 5.5 %collective-permute-start.2 = (bf16[32,128]{1,0:T(8,128)(2,1)S(1)}, bf16[32,128]{1,0:T(8,128)(2,1)S(1)}, u32[]{:S(2)}, u32[]{:S(2)}) collective-permute-start(bf16[32,128]{1,0:T(8,128)(2,1)S(1)} %get-tuple-element.15), channel_id=1, source_target_pairs={{2,0},{3,1},{6,4},{7,5},{10,8},{11,9},{14,12},{15,13},{18,16},{19,... | collective-permute-start | bytes 24584 | tf_op jit(solution)/shard_map/ppermute | solution.py:170
  16.1 7.3 %collective-permute-start.3 = (bf16[32,128]{1,0:T(8,128)(2,1)S(1)}, bf16[32,128]{1,0:T(8,128)(2,1)S(1)}, u32[]{:S(2)}, u32[]{:S(2)}) collective-permute-start(bf16[32,128]{1,0:T(8,128)(2,1)S(1)} %get-tuple-element.16), channel_id=1, source_target_pairs={{10,0},{14,4},{2,8},{6,12},{11,1},{15,5},{3,9},{7,13},{26,16},{30,... | collective-permute-start | bytes 24584 | tf_op jit(solution)/shard_map/ppermute | solution.py:172
where the time goes:
time: 24.3 us; the launch traced here: 24.1 us
  waiting for transfers between devices  9.89 us (41%)
  starting transfers between devices  8.51 us (35%)
  Pallas kernels  4.06 us (17%)
  local copies, waits for them, and re-layouts  1.59 us (7%)
    pallas_call x3, Pallas kernels, call(): pl.pallas_call(kernel, out_shape=outs, scratch_shapes=list(scratch), comp...  4.06 us
    ppermute x1, waiting for transfers between devices, shards(): recv = lax.ppermute(send, 'freq', swap)  3.85 us
    ppermute x1, starting transfers between devices, shards(): recv = lax.ppermute(send, 'freq', swap)  3.12 us
    ppermute x1, waiting for transfers between devices, shards(): recv_halo = lax.ppermute(high_halo, ('freq', 'tm'), cross)  3.1 us
    ppermute x1, waiting for transfers between devices, shards(): keep_halo = lax.ppermute(low_halo, 'tm', back)  2.94 us
    ppermute x1, starting transfers between devices, shards(): recv = lax.ppermute(high, 'freq', swap)  2.82 us
    unnamed x10, local copies, waits for them, and re-layouts  1.59 us
    ppermute x1, starting transfers between devices, shards(): recv_halo = lax.ppermute(high_halo, ('freq', 'tm'), cross)  1.29 us
  transfers between devices with their start and end apart: 4, of which 3 were waited for; matrix products, arithmetic and copies ran while one was open for 0% of the time, Pallas kernels for 0%

commit v1 on v0

v1 whole, which is shorter than its diff:
```python
import functools

import jax
import jax.numpy as jnp
from jax import lax
from jax.experimental import pallas as pl
from jax.experimental.pallas import tpu as pltpu
from jax.sharding import PartitionSpec as P

MAXOFF = 32
SHIFT = 32
LANES = 128
FINE = 8
PLANES = (MAXOFF - 1 + FINE - 1) // FINE + 1


def bit_reversed(count):
    order = [0]
    while len(order) < count:
        order = [2 * r for r in order] + [2 * r + 1 for r in order]
    return order


def own_columns(freq_count, map_ref, del_ref):
    trials = map_ref.shape[1]
    row_block = trials // (2 * freq_count)
    rows = trials // 2
    levels = freq_count.bit_length() - 1
    freq_index = lax.axis_index("freq")
    core_index = lax.axis_index("trial")
    total = jnp.zeros((1, trials), jnp.int32)
    for level in range(levels):
        node = freq_count - (freq_count >> level) + lax.shift_right_logical(freq_index, level + 1)
        bit = lax.shift_right_logical(freq_index, level) & 1
        total = total + del_ref[pl.ds(node, 1), :] * bit
    first = lax.broadcasted_iota(jnp.int32, (8, trials), 0) == 0
    both = jnp.where(
        first, jnp.broadcast_to(map_ref[...], (8, trials)), jnp.broadcast_to(total, (8, trials))
    )
    place = lax.broadcasted_iota(jnp.int32, (8, rows), 1) // row_block
    mine = jnp.zeros((8, rows), jnp.int32)
    for position, r in enumerate(bit_reversed(freq_count)):
        start = ((freq_index ^ r) * 2 + core_index) * row_block
        turn = lax.rem(position * row_block - start + trials, trials)
        mine = jnp.where(place == position, pltpu.roll(both, turn, 1)[:, :rows], mine)
    return mine


def build_taps(off_ref, wt_ref, mine, rhs_ref):
    band, trials = wt_ref.shape
    rows = mine.shape[1]
    picker = mine[0:1, :] == lax.broadcasted_iota(jnp.int32, (trials, rows), 0)
    picker = picker.astype(jnp.float32).astype(jnp.bfloat16)
    tables = jnp.concatenate([wt_ref[...], off_ref[...].astype(jnp.float32).astype(jnp.bfloat16)], axis=0)
    picked = jnp.dot(tables, picker, preferred_element_type=jnp.float32)
    weights = picked[:band]
    lags = picked[band:].astype(jnp.int32) + (mine[1:2, :] & (FINE - 1))
    for fine in range(FINE):
        for plane in range(PLANES):
            rhs_ref[fine * band : (fine + 1) * band, plane * rows : (plane + 1) * rows] = jnp.where(
                lags == plane * FINE + fine, weights, 0.0
            ).astype(jnp.bfloat16)


def convolve(window, span, columns, delay_row, rhs_ref, time_ref, lhs_ref, plane_ref, leaf_ref):
    band = window.shape[0]
    rows = delay_row.shape[1]
    leaf_rows = columns + span
    lhs_rows = leaf_rows + FINE * (PLANES - 1)
    time_rows = lhs_rows + FINE
    turned = jnp.transpose(jnp.concatenate([window] * (LANES // band), axis=0).astype(jnp.float32))
    time_ref[:time_rows, :] = turned[:time_rows, :]
    low_lanes = lax.broadcasted_iota(jnp.int32, (lhs_rows, LANES), 1) < band
    for pair in range(FINE // 2):
        lhs_ref[:lhs_rows, pair * LANES : (pair + 1) * LANES] = jnp.where(
            low_lanes,
            time_ref[2 * pair : 2 * pair + lhs_rows, :],
            time_ref[2 * pair + 1 : 2 * pair + 1 + lhs_rows, :],
        ).astype(jnp.bfloat16)
    plane_ref[:lhs_rows, :] = jnp.dot(lhs_ref[:lhs_rows, :], rhs_ref[...], preferred_element_type=jnp.float32)
    leaf = plane_ref[:leaf_rows, :rows]
    for plane in range(1, PLANES):
        leaf = leaf + plane_ref[plane * FINE : plane * FINE + leaf_rows, plane * rows : (plane + 1) * rows]
    leaf_ref[:leaf_rows, :] = leaf
    steps = [FINE]
    while steps[-1] * 2 <= span:
        steps.append(steps[-1] * 2)
    blocks = []
    for start in range(0, columns, LANES):
        part = leaf_ref[start : start + LANES + span, :]
        for step in reversed(steps):
            length = LANES + sum(s for s in steps if s < step)
            length = min(length, part.shape[0])
            take = jnp.broadcast_to((delay_row & step) != 0, (length, rows))
            moved = part[step : step + length]
            if moved.shape[0] < length:
                moved = jnp.concatenate([moved, jnp.zeros((length - moved.shape[0], rows), jnp.float32)], axis=0)
            part = jnp.where(take, moved, part[:length])
        blocks.append(jnp.transpose(part[:LANES]).astype(jnp.bfloat16))
    return blocks


def main_kernel(
    freq_count, tail, x_ref, off_ref, wt_ref, map_ref, del_ref,
    keep_ref, send_ref, rhs_ref, delay_ref, time_ref, lhs_ref, plane_ref, leaf_ref,
):
    mine = own_columns(freq_count, map_ref, del_ref)
    build_taps(off_ref, wt_ref, mine, rhs_ref)
    delay_ref[...] = mine
    columns = keep_ref.shape[1]
    span = (freq_count.bit_length() - 1) * SHIFT
    half = keep_ref.shape[0]
    blocks = convolve(x_ref[...], span, columns, mine[1:2, :], rhs_ref, time_ref, lhs_ref, plane_ref, leaf_ref)
    for index, block in enumerate(blocks):
        keep_ref[:, index * LANES : (index + 1) * LANES] = block[:half]
        send_ref[:, index * LANES : (index + 1) * LANES] = block[half:]


def tail_kernel(
    freq_count, tail, x_ref, next_ref, rhs_ref, delay_ref, keep_in_ref, send_in_ref,
    keep_ref, send_ref, time_ref, lhs_ref, plane_ref, leaf_ref,
):
    seg = x_ref.shape[1]
    body = seg - tail
    half = keep_ref.shape[0]
    span = (freq_count.bit_length() - 1) * SHIFT
    window = jnp.concatenate([x_ref[:, body:], next_ref[...]], axis=1)
    blocks = convolve(window, span, tail, delay_ref[1:2, :], rhs_ref, time_ref, lhs_ref, plane_ref, leaf_ref)
    keep_ref[:, :body] = keep_in_ref[...]
    send_ref[:, :body] = send_in_ref[...]
    for index, block in enumerate(blocks):
        place = slice(body + index * LANES, body + (index + 1) * LANES)
        keep_ref[:, place] = block[:half]
        send_ref[:, place] = block[half:]


def add_bf16(a, b):
    return (a.astype(jnp.float32) + b.astype(jnp.float32)).astype(jnp.bfloat16)


def merge_kernel(keep_ref, recv_ref, low_ref, high_ref):
    half = low_ref.shape[0]
    low_ref[...] = add_bf16(keep_ref[:half, :], recv_ref[:half, :])
    high_ref[...] = add_bf16(keep_ref[half:, :], recv_ref[half:, :])


def final_kernel(keep_ref, recv_ref, out_ref):
    out_ref[...] = add_bf16(keep_ref[...], recv_ref[...])


def call(kernel, outs, *args, scratch=(), limit=16 << 20):
    return pl.pallas_call(
        kernel,
        out_shape=outs,
        scratch_shapes=list(scratch),
        compiler_params=pltpu.CompilerParams(vmem_limit_bytes=limit),
    )(*args)


def plane_of(*shape):
    return jax.ShapeDtypeStruct(shape, jnp.bfloat16)


def shards(spectra, tap_offsets, tap_weights, trial_map, delays):
    band, seg = spectra.shape
    trials = trial_map.shape[1]
    freq_count = lax.axis_size("freq")
    tm_count = lax.axis_size("tm")
    levels = freq_count.bit_length() - 1
    rows = trials // 2
    half = rows // 2
    span = levels * SHIFT
    tail = -(-(MAXOFF - 1 + span) // LANES) * LANES
    body = seg - tail

    def scratch(columns):
        leaf_rows = columns + span
        lhs_rows = leaf_rows + FINE * (PLANES - 1)
        return (
            pltpu.VMEM((lhs_rows + FINE, LANES), jnp.float32),
            pltpu.VMEM((lhs_rows, FINE * band), jnp.bfloat16),
            pltpu.VMEM((lhs_rows, PLANES * rows), jnp.float32),
            pltpu.VMEM((leaf_rows, rows), jnp.float32),
        )

    back = [(m + 1, m) for m in range(tm_count - 1)]
    following = lax.ppermute(spectra[:, :tail], "tm", back)
    keep, send, taps, columns = call(
        functools.partial(main_kernel, freq_count, tail),
        [plane_of(half, body)] * 2
        + [plane_of(FINE * band, PLANES * rows), jax.ShapeDtypeStruct((8, rows), jnp.int32)],
        spectra,
        jnp.swapaxes(tap_offsets[0], 0, 1),
        jnp.swapaxes(tap_weights[0], 0, 1),
        trial_map,
        delays,
        scratch=scratch(body),
    )
    keep, send = call(
        functools.partial(tail_kernel, freq_count, tail),
        [plane_of(half, seg)] * 2,
        spectra,
        following,
        taps,
        columns,
        keep,
        send,
        scratch=scratch(tail),
    )
    for level in range(levels):
        swap = [(i, i ^ (1 << level)) for i in range(freq_count)]
        recv = lax.ppermute(send, "freq", swap)
        if level < levels - 1:
            half = keep.shape[0] // 2
            keep, send = call(merge_kernel, [plane_of(half, seg)] * 2, keep, recv)
    return call(final_kernel, plane_of(*keep.shape), keep, recv)


def solution(mesh):
    return jax.shard_map(
        shards,
        mesh=mesh,
        in_specs=(
            P(("beam", "freq"), "tm"),
            P("freq", None, None),
            P("freq", None, None),
            P("freq", None),
            P(),
        ),
        out_specs=P(("beam", "freq", "trial"), "tm"),
        check_vma=False,
    )
```

time: 24.3 us -> 20.2 us (0.83)
  the two profiles are of different devices: /device:TPU:0 before, /device:TPU:26 now
where the time goes in v1:
time: 20.2 us; the launch traced here: 19.9 us
  waiting for transfers between devices  9.94 us (49%)
  local copies, waits for them, and re-layouts  3.82 us (19%)
  starting transfers between devices  3.34 us (17%)
  Pallas kernels  2.72 us (13%)
    ppermute x2, waiting for transfers between devices, shards(): recv = lax.ppermute(send, 'freq', swap)  9.94 us
    unnamed x10, local copies, waits for them, and re-layouts  3.1 us
    pallas_call x4, Pallas kernels, call(): pl.pallas_call(kernel, out_shape=outs, scratch_shapes=list(scratch), comp...  2.72 us
    ppermute x1, starting transfers between devices, shards(): following = lax.ppermute(spectra[:, :tail], 'tm', back)  2.43 us
    ppermute x2, starting transfers between devices, shards(): recv = lax.ppermute(send, 'freq', swap)  0.91 us
    slice x1, local copies, waits for them, and re-layouts, shards(): following = lax.ppermute(spectra[:, :tail], 'tm', back)  0.73 us
  transfers between devices with their start and end apart: 3, of which 2 were waited for; matrix products, arithmetic and copies ran while one was open for 0% of the time, Pallas kernels for 8%

profile of v1, /device:TPU:26, one launch (start us, length us, event | category | flops | bytes accessed | tf_op | source)
XLA Modules:
  0.0 19.9 jit_solution(14844437160049874750)
XLA Ops:
  0.0 0.0 copy-start.2
  0.0 0.7 %slice.3 = bf16[64,128]{1,0:T(8,128)(2,1)S(1)} slice(bf16[64,1024]{1,0:T(8,128)(2,1)} %x_ref.3), slice={[0:64], [0:128]} | slice | bytes 32768 | tf_op jit(solution)/shard_map/slice | solution.py:187
  0.7 2.4 %collective-permute-start = (bf16[64,128]{1,0:T(8,128)(2,1)S(1)}, bf16[64,128]{1,0:T(8,128)(2,1)S(1)}, u32[]{:S(2)}, u32[]{:S(2)}) collective-permute-start(bf16[64,128]{1,0:T(8,128)(2,1)S(1)} %slice.3), channel_id=1, source_target_pairs={{2,0},{3,1},{6,4},{7,5},{10,8},{11,9},{14,12},{15,13},{18,16},{19,... | collective-permute-start | bytes 49160 | tf_op jit(solution)/shard_map/ppermute | solution.py:187
  3.2 0.0 copy-start.4
  3.2 0.0 copy-done.2
  3.2 0.7 %copy-done.4 = s32[1,256]{1,0:T(1,128)S(1)} copy-done((s32[1,256]{1,0:T(1,128)S(1)}, s32[1,256]{1,0:T(1,128)}, u32[]{:S(2)}) %copy-start.4) | copy-done | bytes 1048
  3.8 0.0 copy-start
  3.8 0.9 %copy-done = bf16[64,1024]{1,0:T(8,128)(2,1)S(1)} copy-done((bf16[64,1024]{1,0:T(8,128)(2,1)S(1)}, bf16[64,1024]{1,0:T(8,128)(2,1)}, u32[]{:S(2)}) %copy-start) | copy-done | bytes 131096
  4.8 0.0 copy-start.1
  4.8 0.8 %copy-done.1 = s32[1,256,64]{1,2,0:T(8,128)S(1)} copy-done((s32[1,256,64]{1,2,0:T(8,128)S(1)}, s32[1,256,64]{1,2,0:T(8,128)}, u32[]{:S(2)}) %copy-start.1) | copy-done | bytes 65560
  5.6 0.0 copy-start.3
  5.6 0.7 %copy-done.3 = s32[3,256]{1,0:T(4,128)S(1)} copy-done((s32[3,256]{1,0:T(4,128)S(1)}, s32[3,256]{1,0:T(4,128)}, u32[]{:S(2)}) %copy-start.3) | copy-done | bytes 3096
  6.3 1.5 %shard_map.55 = (bf16[64,896]{1,0:T(8,128)(2,1)S(1)}, bf16[64,896]{1,0:T(8,128)(2,1)S(1)}, bf16[512,640]{1,0:T(8,128)(2,1)S(1)}, s32[8,128]{1,0:T(8,128)S(1)}) custom-call(bf16[64,1024]{1,0:T(8,128)(2,1)S(1)} %copy-done, s32[64,256]{1,0:T(8,128)S(1)} %bitcast.6, bf16[64,256]{1,0:T(8,128)(2,1)S(1)} %bitcast.7, s32[1,256]{1,0:T(1,128)S(1)} %copy-done.4, ...), custom_call_target="tpu_custom_call" | custom-call | tf_op jit(solution)/shard_map/pallas_call | solution.py:152
  7.8 0.0 collective-permute-done.next_ref
  7.8 0.5 %shard_map.56 = (bf16[64,1024]{1,0:T(8,128)(2,1)S(1)}, bf16[64,1024]{1,0:T(8,128)(2,1)S(1)}) custom-call(bf16[64,1024]{1,0:T(8,128)(2,1)S(1)} %copy-done, bf16[64,128]{1,0:T(8,128)(2,1)S(1)} %collective-permute-done.next_ref, bf16[512,640]{1,0:T(8,128)(2,1)S(1)} %get-tuple-element.13.rhs_ref, s32[8,128]{1,0:T(8,128)S(1)} %get-tuple-element.14.delay_ref, ...), custom_call_target="tpu_custom_call" | custom-call | tf_op jit(solution)/shard_map/pallas_call | solution.py:152
  8.3 0.5 %collective-permute-start.1 = (bf16[64,1024]{1,0:T(8,128)(2,1)S(1)}, bf16[64,1024]{1,0:T(8,128)(2,1)S(1)}, u32[]{:S(2)}, u32[]{:S(2)}) collective-permute-start(bf16[64,1024]{1,0:T(8,128)(2,1)S(1)} %get-tuple-element.18), channel_id=1, source_target_pairs={{0,4},{4,0},{8,12},{12,8},{1,5},{5,1},{9,13},{13,9},{2,6},{6,2},{1... | collective-permute-start | bytes 393224 | tf_op jit(solution)/shard_map/ppermute | solution.py:212
  8.9 4.5 %collective-permute-done.1.recv_ref = bf16[64,1024]{1,0:T(8,128)(2,1)S(1)} collective-permute-done((bf16[64,1024]{1,0:T(8,128)(2,1)S(1)}, bf16[64,1024]{1,0:T(8,128)(2,1)S(1)}, u32[]{:S(2)}, u32[]{:S(2)}) %collective-permute-start.1) | collective-permute-done | bytes 131104 | tf_op jit(solution)/shard_map/ppermute | solution.py:212
  13.4 0.4 %collective-permute-start.2 = (bf16[32,1024]{1,0:T(8,128)(2,1)S(1)}, bf16[32,1024]{1,0:T(8,128)(2,1)S(1)}, u32[]{:S(2)}, u32[]{:S(2)}) collective-permute-start(bf16[32,1024]{1,0:T(8,128)(2,1)S(1)} %get-tuple-element.20), channel_id=1, source_target_pairs={{0,8},{4,12},{8,0},{12,4},{1,9},{5,13},{9,1},{13,5},{2,10},{6,14},... | collective-permute-start | bytes 196616 | tf_op jit(solution)/shard_map/ppermute | solution.py:212
  13.8 5.4 %collective-permute-done.2.recv_ref = bf16[32,1024]{1,0:T(8,128)(2,1)S(1)} collective-permute-done((bf16[32,1024]{1,0:T(8,128)(2,1)S(1)}, bf16[32,1024]{1,0:T(8,128)(2,1)S(1)}, u32[]{:S(2)}, u32[]{:S(2)}) %collective-permute-start.2) | collective-permute-done | bytes 65568 | tf_op jit(solution)/shard_map/ppermute | solution.py:212
  19.2 0.6 %shard_map.58 = bf16[32,1024]{1,0:T(8,128)(2,1)} custom-call(bf16[32,1024]{1,0:T(8,128)(2,1)S(1)} %get-tuple-element.19.keep_ref, bf16[32,1024]{1,0:T(8,128)(2,1)S(1)} %collective-permute-done.2.recv_ref), custom_call_target="tpu_custom_call" | custom-call | tf_op jit(solution)/shard_map/pallas_call | solution.py:152
  (1 shorter events, 0.0 us)
Async XLA Ops:
  0.0 3.2 %copy-start.2 = (bf16[1,256,64]{1,2,0:T(8,128)(2,1)S(1)}, bf16[1,256,64]{1,2,0:T(8,128)(2,1)}, u32[]{:S(2)}) copy-start(bf16[1,256,64]{1,2,0:T(8,128)(2,1)} %param.7) | copy-start | bytes 98308
  0.7 7.1 %collective-permute-start = (bf16[64,128]{1,0:T(8,128)(2,1)S(1)}, bf16[64,128]{1,0:T(8,128)(2,1)S(1)}, u32[]{:S(2)}, u32[]{:S(2)}) collective-permute-start(bf16[64,128]{1,0:T(8,128)(2,1)S(1)} %slice.3), channel_id=1, source_target_pairs={{2,0},{3,1},{6,4},{7,5},{10,8},{11,9},{14,12},{15,13},{18,16},{19,... | collective-permute-start | bytes 49160 | tf_op jit(solution)/shard_map/ppermute | solution.py:187
  3.2 0.7 %copy-start.4 = (s32[1,256]{1,0:T(1,128)S(1)}, s32[1,256]{1,0:T(1,128)}, u32[]{:S(2)}) copy-start(s32[1,256]{1,0:T(1,128)} %map_ref.1) | copy-start | bytes 3076
  3.8 0.9 %copy-start = (bf16[64,1024]{1,0:T(8,128)(2,1)S(1)}, bf16[64,1024]{1,0:T(8,128)(2,1)}, u32[]{:S(2)}) copy-start(bf16[64,1024]{1,0:T(8,128)(2,1)} %x_ref.3) | copy-start | bytes 393220
  4.8 0.8 %copy-start.1 = (s32[1,256,64]{1,2,0:T(8,128)S(1)}, s32[1,256,64]{1,2,0:T(8,128)}, u32[]{:S(2)}) copy-start(s32[1,256,64]{1,2,0:T(8,128)} %param.6) | copy-start | bytes 196612
  5.6 0.7 %copy-start.3 = (s32[3,256]{1,0:T(4,128)S(1)}, s32[3,256]{1,0:T(4,128)}, u32[]{:S(2)}) copy-start(s32[3,256]{1,0:T(4,128)} %del_ref.1) | copy-start | bytes 9220
  8.3 5.0 %collective-permute-start.1 = (bf16[64,1024]{1,0:T(8,128)(2,1)S(1)}, bf16[64,1024]{1,0:T(8,128)(2,1)S(1)}, u32[]{:S(2)}, u32[]{:S(2)}) collective-permute-start(bf16[64,1024]{1,0:T(8,128)(2,1)S(1)} %get-tuple-element.18), channel_id=1, source_target_pairs={{0,4},{4,0},{8,12},{12,8},{1,5},{5,1},{9,13},{13,9},{2,6},{6,2},{1... | collective-permute-start | bytes 393224 | tf_op jit(solution)/shard_map/ppermute | solution.py:212
  13.4 5.8 %collective-permute-start.2 = (bf16[32,1024]{1,0:T(8,128)(2,1)S(1)}, bf16[32,1024]{1,0:T(8,128)(2,1)S(1)}, u32[]{:S(2)}, u32[]{:S(2)}) collective-permute-start(bf16[32,1024]{1,0:T(8,128)(2,1)S(1)} %get-tuple-element.20), channel_id=1, source_target_pairs={{0,8},{4,12},{8,0},{12,4},{1,9},{5,13},{9,1},{13,5},{2,10},{6,14},... | collective-permute-start | bytes 196616 | tf_op jit(solution)/shard_map/ppermute | solution.py:212

commit v2 on v1

--- a/solution.py
+++ b/solution.py
@@ -101,11 +101,25 @@
 
 
 def main_kernel(
-    freq_count, tail, x_ref, off_ref, wt_ref, map_ref, del_ref,
-    keep_ref, send_ref, rhs_ref, delay_ref, time_ref, lhs_ref, plane_ref, leaf_ref,
+    freq_count, tail, x_hbm, off_hbm, wt_hbm, map_hbm, del_hbm,
+    keep_ref, send_ref, rhs_ref, delay_ref, x_ref,
+    off_ref, wt_ref, map_ref, del_ref, time_ref, lhs_ref, plane_ref, leaf_ref, sems,
 ):
+    moves = [
+        pltpu.make_async_copy(source, target, sems.at[index])
+        for index, (source, target) in enumerate(
+            ((map_hbm, map_ref), (del_hbm, del_ref), (wt_hbm, wt_ref), (off_hbm, off_ref), (x_hbm, x_ref))
+        )
+    ]
+    for move in moves:
+        move.start()
+    moves[0].wait()
+    moves[1].wait()
     mine = own_columns(freq_count, map_ref, del_ref)
+    moves[2].wait()
+    moves[3].wait()
     build_taps(off_ref, wt_ref, mine, rhs_ref)
+    moves[4].wait()
     delay_ref[...] = mine
     columns = keep_ref.shape[1]
     span = (freq_count.bit_length() - 1) * SHIFT
@@ -117,14 +131,16 @@
 
 
 def tail_kernel(
-    freq_count, tail, x_ref, next_ref, rhs_ref, delay_ref, keep_in_ref, send_in_ref,
+    freq_count, tail, tm_count, x_ref, next_ref, rhs_ref, delay_ref, keep_in_ref, send_in_ref,
     keep_ref, send_ref, time_ref, lhs_ref, plane_ref, leaf_ref,
 ):
     seg = x_ref.shape[1]
     body = seg - tail
     half = keep_ref.shape[0]
     span = (freq_count.bit_length() - 1) * SHIFT
-    window = jnp.concatenate([x_ref[:, body:], next_ref[...]], axis=1)
+    inside = lax.axis_index("tm") < tm_count - 1
+    following = jnp.where(inside, next_ref[:, :tail].astype(jnp.float32), 0.0).astype(jnp.bfloat16)
+    window = jnp.concatenate([x_ref[:, body:], following], axis=1)
     blocks = convolve(window, span, tail, delay_ref[1:2, :], rhs_ref, time_ref, lhs_ref, plane_ref, leaf_ref)
     keep_ref[:, :body] = keep_in_ref[...]
     send_ref[:, :body] = send_in_ref[...]
@@ -148,10 +164,14 @@
     out_ref[...] = add_bf16(keep_ref[...], recv_ref[...])
 
 
-def call(kernel, outs, *args, scratch=(), limit=16 << 20):
+def call(kernel, outs, *args, scratch=(), limit=16 << 20, space=None):
+    specs = {} if space is None else {"in_specs": [pl.BlockSpec(memory_space=space)] * len(args)}
+    if space is not None:
+        args = [pltpu.with_memory_space_constraint(arg, space) for arg in args]
     return pl.pallas_call(
         kernel,
         out_shape=outs,
+        **specs,
         scratch_shapes=list(scratch),
         compiler_params=pltpu.CompilerParams(vmem_limit_bytes=limit),
     )(*args)
@@ -183,23 +203,35 @@
             pltpu.VMEM((leaf_rows, rows), jnp.float32),
         )
 
-    back = [(m + 1, m) for m in range(tm_count - 1)]
-    following = lax.ppermute(spectra[:, :tail], "tm", back)
-    keep, send, taps, columns = call(
+    ring = [((m + 1) % tm_count, m) for m in range(tm_count)]
+    following = lax.ppermute(spectra, "tm", ring)
+    keep, send, taps, columns, samples = call(
         functools.partial(main_kernel, freq_count, tail),
         [plane_of(half, body)] * 2
-        + [plane_of(FINE * band, PLANES * rows), jax.ShapeDtypeStruct((8, rows), jnp.int32)],
+        + [
+            plane_of(FINE * band, PLANES * rows),
+            jax.ShapeDtypeStruct((8, rows), jnp.int32),
+            plane_of(band, seg),
+        ],
         spectra,
         jnp.swapaxes(tap_offsets[0], 0, 1),
         jnp.swapaxes(tap_weights[0], 0, 1),
         trial_map,
         delays,
-        scratch=scratch(body),
+        scratch=(
+            pltpu.VMEM((band, trials), jnp.int32),
+            pltpu.VMEM((band, trials), jnp.bfloat16),
+            pltpu.VMEM((1, trials), jnp.int32),
+            pltpu.VMEM(delays.shape, jnp.int32),
+        )
+        + scratch(body)
+        + (pltpu.SemaphoreType.DMA((5,)),),
+        space=pltpu.HBM,
     )
     keep, send = call(
-        functools.partial(tail_kernel, freq_count, tail),
+        functools.partial(tail_kernel, freq_count, tail, tm_count),
         [plane_of(half, seg)] * 2,
-        spectra,
+        samples,
         following,
         taps,
         columns,

time: 20.2 us -> 18.3 us (0.906)
  the two profiles are of different devices: /device:TPU:26 before, /device:TPU:0 now
where the time goes in v2:
time: 18.3 us; the launch traced here: 18.1 us
  starting transfers between devices  7.77 us (42%)
  waiting for transfers between devices  6.71 us (37%)
  Pallas kernels  3.63 us (20%)
    ppermute x2, waiting for transfers between devices, shards(): recv = lax.ppermute(send, 'freq', swap)  5.46 us
    ppermute x2, starting transfers between devices, shards(): recv = lax.ppermute(send, 'freq', swap)  4.8 us
    pallas_call x4, Pallas kernels, call(): pl.pallas_call(kernel, out_shape=outs, **specs, scratch_shapes=list(scrat...  3.63 us
    ppermute x1, starting transfers between devices, shards(): following = lax.ppermute(spectra, 'tm', ring)  2.97 us
    ppermute x1, waiting for transfers between devices, shards(): following = lax.ppermute(spectra, 'tm', ring)  1.25 us
  transfers between devices with their start and end apart: 3, of which 3 were waited for; matrix products, arithmetic and copies ran while one was open for 0% of the time, Pallas kernels for 14%

profile of v2, /device:TPU:0, one launch (start us, length us, event | category | flops | bytes accessed | tf_op | source)
XLA Modules:
  0.0 18.1 jit_solution(15655793008130391130)
XLA Ops:
  0.0 3.0 %collective-permute-start = (bf16[64,1024]{1,0:T(8,128)(2,1)}, bf16[64,1024]{1,0:T(8,128)(2,1)S(1)}, u32[]{:S(2)}, u32[]{:S(2)}) collective-permute-start(bf16[64,1024]{1,0:T(8,128)(2,1)} %x_hbm.1), channel_id=1, source_target_pairs={{2,0},{0,2},{3,1},{1,3},{6,4},{4,6},{7,5},{5,7},{10,8},{8,10},{11,... | collective-permute-start | bytes 393224 | tf_op jit(solution)/shard_map/ppermute | solution.py:207
  3.0 2.4 %shard_map.55 = (bf16[64,896]{1,0:T(8,128)(2,1)S(1)}, bf16[64,896]{1,0:T(8,128)(2,1)S(1)}, bf16[512,640]{1,0:T(8,128)(2,1)S(1)}, s32[8,128]{1,0:T(8,128)S(1)}, bf16[64,1024]{1,0:T(8,128)(2,1)S(1)}) custom-call(bf16[64,1024]{1,0:T(8,128)(2,1)} %x_hbm.1, s32[64,256]{1,0:T(8,128)} %bitcast.6, bf16[64,256]{1,0:T(8,128)(2,1)} %bitcast.7, s32[1,256]{1,0:T(1,128)} %map_hbm.1, ...), custom_call_target="tpu_custom_call" | custom-call | tf_op jit(solution)/shard_map/pallas_call | solution.py:171
  5.4 1.3 %collective-permute-done.next_ref = bf16[64,1024]{1,0:T(8,128)(2,1)S(1)} collective-permute-done((bf16[64,1024]{1,0:T(8,128)(2,1)}, bf16[64,1024]{1,0:T(8,128)(2,1)S(1)}, u32[]{:S(2)}, u32[]{:S(2)}) %collective-permute-start) | collective-permute-done | bytes 131104 | tf_op jit(solution)/shard_map/ppermute | solution.py:207
  6.7 0.5 %shard_map.56 = (bf16[64,1024]{1,0:T(8,128)(2,1)S(1)}, bf16[64,1024]{1,0:T(8,128)(2,1)S(1)}) custom-call(bf16[64,1024]{1,0:T(8,128)(2,1)S(1)} %get-tuple-element.14.x_ref, bf16[64,1024]{1,0:T(8,128)(2,1)S(1)} %collective-permute-done.next_ref, bf16[512,640]{1,0:T(8,128)(2,1)S(1)} %get-tuple-element.15.rhs_ref, s32[8,128]{1,0:T(8,128)S(1)} %get-tuple-element.16.delay_ref, ...), custom_call_target="tpu_custom_call" | custom-call | tf_op jit(solution)/shard_map/pallas_call | solution.py:171
  7.2 1.9 %collective-permute-start.1 = (bf16[64,1024]{1,0:T(8,128)(2,1)S(1)}, bf16[64,1024]{1,0:T(8,128)(2,1)S(1)}, u32[]{:S(2)}, u32[]{:S(2)}) collective-permute-start(bf16[64,1024]{1,0:T(8,128)(2,1)S(1)} %get-tuple-element.20), channel_id=1, source_target_pairs={{0,4},{4,0},{8,12},{12,8},{1,5},{5,1},{9,13},{13,9},{2,6},{6,2},{1... | collective-permute-start | bytes 393224 | tf_op jit(solution)/shard_map/ppermute | solution.py:244
  9.1 3.1 %collective-permute-done.1.recv_ref = bf16[64,1024]{1,0:T(8,128)(2,1)S(1)} collective-permute-done((bf16[64,1024]{1,0:T(8,128)(2,1)S(1)}, bf16[64,1024]{1,0:T(8,128)(2,1)S(1)}, u32[]{:S(2)}, u32[]{:S(2)}) %collective-permute-start.1) | collective-permute-done | bytes 131104 | tf_op jit(solution)/shard_map/ppermute | solution.py:244
  12.3 2.9 %collective-permute-start.2 = (bf16[32,1024]{1,0:T(8,128)(2,1)S(1)}, bf16[32,1024]{1,0:T(8,128)(2,1)S(1)}, u32[]{:S(2)}, u32[]{:S(2)}) collective-permute-start(bf16[32,1024]{1,0:T(8,128)(2,1)S(1)} %get-tuple-element.22), channel_id=1, source_target_pairs={{0,8},{4,12},{8,0},{12,4},{1,9},{5,13},{9,1},{13,5},{2,10},{6,14},... | collective-permute-start | bytes 196616 | tf_op jit(solution)/shard_map/ppermute | solution.py:244
  15.2 2.3 %collective-permute-done.2.recv_ref = bf16[32,1024]{1,0:T(8,128)(2,1)S(1)} collective-permute-done((bf16[32,1024]{1,0:T(8,128)(2,1)S(1)}, bf16[32,1024]{1,0:T(8,128)(2,1)S(1)}, u32[]{:S(2)}, u32[]{:S(2)}) %collective-permute-start.2) | collective-permute-done | bytes 65568 | tf_op jit(solution)/shard_map/ppermute | solution.py:244
  17.5 0.6 %shard_map.58 = bf16[32,1024]{1,0:T(8,128)(2,1)} custom-call(bf16[32,1024]{1,0:T(8,128)(2,1)S(1)} %get-tuple-element.21.keep_ref, bf16[32,1024]{1,0:T(8,128)(2,1)S(1)} %collective-permute-done.2.recv_ref), custom_call_target="tpu_custom_call" | custom-call | tf_op jit(solution)/shard_map/pallas_call | solution.py:171
  (1 shorter events, 0.0 us)
Async XLA Ops:
  0.0 6.7 %collective-permute-start = (bf16[64,1024]{1,0:T(8,128)(2,1)}, bf16[64,1024]{1,0:T(8,128)(2,1)S(1)}, u32[]{:S(2)}, u32[]{:S(2)}) collective-permute-start(bf16[64,1024]{1,0:T(8,128)(2,1)} %x_hbm.1), channel_id=1, source_target_pairs={{2,0},{0,2},{3,1},{1,3},{6,4},{4,6},{7,5},{5,7},{10,8},{8,10},{11,... | collective-permute-start | bytes 393224 | tf_op jit(solution)/shard_map/ppermute | solution.py:207
  7.2 5.0 %collective-permute-start.1 = (bf16[64,1024]{1,0:T(8,128)(2,1)S(1)}, bf16[64,1024]{1,0:T(8,128)(2,1)S(1)}, u32[]{:S(2)}, u32[]{:S(2)}) collective-permute-start(bf16[64,1024]{1,0:T(8,128)(2,1)S(1)} %get-tuple-element.20), channel_id=1, source_target_pairs={{0,4},{4,0},{8,12},{12,8},{1,5},{5,1},{9,13},{13,9},{2,6},{6,2},{1... | collective-permute-start | bytes 393224 | tf_op jit(solution)/shard_map/ppermute | solution.py:244
  12.3 5.2 %collective-permute-start.2 = (bf16[32,1024]{1,0:T(8,128)(2,1)S(1)}, bf16[32,1024]{1,0:T(8,128)(2,1)S(1)}, u32[]{:S(2)}, u32[]{:S(2)}) collective-permute-start(bf16[32,1024]{1,0:T(8,128)(2,1)S(1)} %get-tuple-element.22), channel_id=1, source_target_pairs={{0,8},{4,12},{8,0},{12,4},{1,9},{5,13},{9,1},{13,5},{2,10},{6,14},... | collective-permute-start | bytes 196616 | tf_op jit(solution)/shard_map/ppermute | solution.py:244

commit v3 on v1

--- a/solution.py
+++ b/solution.py
@@ -100,58 +100,82 @@
     return blocks
 
 
+def load_kernel(x_hbm, off_hbm, wt_hbm, map_hbm, del_hbm, edge_ref, x_ref, off_ref, wt_ref, map_ref, del_ref, sems):
+    moves = [
+        pltpu.make_async_copy(source, target, sems.at[index])
+        for index, (source, target) in enumerate(
+            (
+                (x_hbm.at[:, : edge_ref.shape[1]], edge_ref),
+                (x_hbm, x_ref),
+                (off_hbm, off_ref),
+                (wt_hbm, wt_ref),
+                (map_hbm, map_ref),
+                (del_hbm, del_ref),
+            )
+        )
+    ]
+    for move in moves:
+        move.start()
+    for move in moves:
+        move.wait()
+
+
 def main_kernel(
-    freq_count, tail, x_ref, off_ref, wt_ref, map_ref, del_ref,
-    keep_ref, send_ref, rhs_ref, delay_ref, time_ref, lhs_ref, plane_ref, leaf_ref,
+    freq_count, x_ref, off_ref, wt_ref, map_ref, del_ref,
+    body_ref, rhs_ref, delay_ref, time_ref, lhs_ref, plane_ref, leaf_ref,
 ):
     mine = own_columns(freq_count, map_ref, del_ref)
     build_taps(off_ref, wt_ref, mine, rhs_ref)
     delay_ref[...] = mine
-    columns = keep_ref.shape[1]
+    columns = body_ref.shape[1]
     span = (freq_count.bit_length() - 1) * SHIFT
-    half = keep_ref.shape[0]
     blocks = convolve(x_ref[...], span, columns, mine[1:2, :], rhs_ref, time_ref, lhs_ref, plane_ref, leaf_ref)
     for index, block in enumerate(blocks):
-        keep_ref[:, index * LANES : (index + 1) * LANES] = block[:half]
-        send_ref[:, index * LANES : (index + 1) * LANES] = block[half:]
+        body_ref[:, index * LANES : (index + 1) * LANES] = block
 
 
 def tail_kernel(
-    freq_count, tail, x_ref, next_ref, rhs_ref, delay_ref, keep_in_ref, send_in_ref,
-    keep_ref, send_ref, time_ref, lhs_ref, plane_ref, leaf_ref,
+    freq_count, tm_count, parts, x_ref, next_ref, rhs_ref, delay_ref, body_ref, *rest
 ):
-    seg = x_ref.shape[1]
-    body = seg - tail
-    half = keep_ref.shape[0]
+    outs, (time_ref, lhs_ref, plane_ref, leaf_ref) = rest[:parts], rest[parts:]
+    body = body_ref.shape[1]
+    tail = x_ref.shape[1] - body
+    piece = outs[0].shape[0]
     span = (freq_count.bit_length() - 1) * SHIFT
-    window = jnp.concatenate([x_ref[:, body:], next_ref[...]], axis=1)
+    inside = lax.axis_index("tm") < tm_count - 1
+    following = jnp.where(inside, next_ref[...].astype(jnp.float32), 0.0).astype(jnp.bfloat16)
+    window = jnp.concatenate([x_ref[:, body:], following], axis=1)
     blocks = convolve(window, span, tail, delay_ref[1:2, :], rhs_ref, time_ref, lhs_ref, plane_ref, leaf_ref)
-    keep_ref[:, :body] = keep_in_ref[...]
-    send_ref[:, :body] = send_in_ref[...]
-    for index, block in enumerate(blocks):
-        place = slice(body + index * LANES, body + (index + 1) * LANES)
-        keep_ref[:, place] = block[:half]
-        send_ref[:, place] = block[half:]
+    for part, out_ref in enumerate(outs):
+        rows = slice(part * piece, (part + 1) * piece)
+        out_ref[:, :body] = body_ref[rows, :]
+        for index, block in enumerate(blocks):
+            out_ref[:, body + index * LANES : body + (index + 1) * LANES] = block[rows]
 
 
 def add_bf16(a, b):
     return (a.astype(jnp.float32) + b.astype(jnp.float32)).astype(jnp.bfloat16)
 
 
-def merge_kernel(keep_ref, recv_ref, low_ref, high_ref):
-    half = low_ref.shape[0]
-    low_ref[...] = add_bf16(keep_ref[:half, :], recv_ref[:half, :])
-    high_ref[...] = add_bf16(keep_ref[half:, :], recv_ref[half:, :])
+def merge_kernel(keep_ref, recv_ref, *outs):
+    piece = outs[0].shape[0]
+    for part, out_ref in enumerate(outs):
+        rows = slice(part * piece, (part + 1) * piece)
+        out_ref[...] = add_bf16(keep_ref[rows, :], recv_ref[rows, :])
 
 
 def final_kernel(keep_ref, recv_ref, out_ref):
     out_ref[...] = add_bf16(keep_ref[...], recv_ref[...])
 
 
-def call(kernel, outs, *args, scratch=(), limit=16 << 20):
+def call(kernel, outs, *args, scratch=(), limit=16 << 20, space=None):
+    specs = {} if space is None else {"in_specs": [pl.BlockSpec(memory_space=space)] * len(args)}
+    if space is not None:
+        args = [pltpu.with_memory_space_constraint(arg, space) for arg in args]
     return pl.pallas_call(
         kernel,
         out_shape=outs,
+        **specs,
         scratch_shapes=list(scratch),
         compiler_params=pltpu.CompilerParams(vmem_limit_bytes=limit),
     )(*args)
@@ -168,7 +192,6 @@
     tm_count = lax.axis_size("tm")
     levels = freq_count.bit_length() - 1
     rows = trials // 2
-    half = rows // 2
     span = levels * SHIFT
     tail = -(-(MAXOFF - 1 + span) // LANES) * LANES
     body = seg - tail
@@ -183,36 +206,63 @@
             pltpu.VMEM((leaf_rows, rows), jnp.float32),
         )
 
-    back = [(m + 1, m) for m in range(tm_count - 1)]
-    following = lax.ppermute(spectra[:, :tail], "tm", back)
-    keep, send, taps, columns = call(
-        functools.partial(main_kernel, freq_count, tail),
-        [plane_of(half, body)] * 2
-        + [plane_of(FINE * band, PLANES * rows), jax.ShapeDtypeStruct((8, rows), jnp.int32)],
+    edge, samples, lags, weights, chosen, lateness = call(
+        load_kernel,
+        [
+            plane_of(band, tail),
+            plane_of(band, seg),
+            jax.ShapeDtypeStruct((band, trials), jnp.int32),
+            plane_of(band, trials),
+            jax.ShapeDtypeStruct((1, trials), jnp.int32),
+            jax.ShapeDtypeStruct(delays.shape, jnp.int32),
+        ],
         spectra,
         jnp.swapaxes(tap_offsets[0], 0, 1),
         jnp.swapaxes(tap_weights[0], 0, 1),
         trial_map,
         delays,
+        scratch=(pltpu.SemaphoreType.DMA((6,)),),
+        space=pltpu.HBM,
+    )
+    ring = [((m + 1) % tm_count, m) for m in range(tm_count)]
+    following = lax.ppermute(edge, "tm", ring)
+    planes, taps, columns = call(
+        functools.partial(main_kernel, freq_count),
+        [
+            plane_of(rows, body),
+            plane_of(FINE * band, PLANES * rows),
+            jax.ShapeDtypeStruct((8, rows), jnp.int32),
+        ],
+        samples,
+        lags,
+        weights,
+        chosen,
+        lateness,
         scratch=scratch(body),
     )
-    keep, send = call(
-        functools.partial(tail_kernel, freq_count, tail),
-        [plane_of(half, seg)] * 2,
-        spectra,
+    parts = 4 if levels > 1 else 2
+    pieces = call(
+        functools.partial(tail_kernel, freq_count, tm_count, parts),
+        [plane_of(rows // parts, seg)] * parts,
+        samples,
         following,
         taps,
         columns,
-        keep,
-        send,
+        planes,
         scratch=scratch(tail),
     )
-    for level in range(levels):
+    for level in range(levels - 1):
         swap = [(i, i ^ (1 << level)) for i in range(freq_count)]
-        recv = lax.ppermute(send, "freq", swap)
-        if level < levels - 1:
-            half = keep.shape[0] // 2
-            keep, send = call(merge_kernel, [plane_of(half, seg)] * 2, keep, recv)
+        keep_first, keep_next, send_first, send_next = pieces
+        count = 1 if level == levels - 2 else 2
+        shapes = [plane_of(keep_first.shape[0] // count, seg)] * count
+        early = lax.ppermute(send_next, "freq", swap)
+        late = lax.ppermute(send_first, "freq", swap)
+        forwarded = call(merge_kernel, shapes, keep_next, early)
+        kept = call(merge_kernel, shapes, keep_first, late)
+        pieces = [*kept, *forwarded]
+    keep, send = pieces
+    recv = lax.ppermute(send, "freq", [(i, i ^ (1 << (levels - 1))) for i in range(freq_count)])
     return call(final_kernel, plane_of(*keep.shape), keep, recv)
 
 

time: 20.2 us -> 17.1 us (0.85)
  the two profiles are of different devices: /device:TPU:26 before, /device:TPU:0 now
where the time goes in v3:
time: 17.1 us; the launch traced here: 16.9 us
  starting transfers between devices  8.07 us (47%)
  waiting for transfers between devices  5.1 us (30%)
  Pallas kernels  3.75 us (22%)
    pallas_call x6, Pallas kernels, call(): pl.pallas_call(kernel, out_shape=outs, **specs, scratch_shapes=list(scrat...  3.75 us
    ppermute x1, starting transfers between devices, shards(): following = lax.ppermute(edge, 'tm', ring)  3.03 us
    ppermute x1, starting transfers between devices, shards(): lax.ppermute(send, 'freq', [(i, i ^ 1 << levels - 1) for i in range(freq_...  2.79 us
    ppermute x1, waiting for transfers between devices, shards(): early = lax.ppermute(send_next, 'freq', swap)  2.48 us
    ppermute x1, waiting for transfers between devices, shards(): lax.ppermute(send, 'freq', [(i, i ^ 1 << levels - 1) for i in range(freq_...  2.42 us
    ppermute x1, starting transfers between devices, shards(): early = lax.ppermute(send_next, 'freq', swap)  2.17 us
  transfers between devices with their start and end apart: 4, of which 3 were waited for; matrix products, arithmetic and copies ran while one was open for 0% of the time, Pallas kernels for 9%

profile of v3, /device:TPU:0, one launch (start us, length us, event | category | flops | bytes accessed | tf_op | source)
XLA Modules:
  0.0 16.9 jit_solution(11570038061774020164)
XLA Ops:
  0.0 1.0 %shard_map.55 = (bf16[64,128]{1,0:T(8,128)(2,1)S(1)}, bf16[64,1024]{1,0:T(8,128)(2,1)S(1)}, s32[64,256]{1,0:T(8,128)S(1)}, bf16[64,256]{1,0:T(8,128)(2,1)S(1)}, ...) custom-call(bf16[64,1024]{1,0:T(8,128)(2,1)} %x_hbm.1, s32[64,256]{1,0:T(8,128)} %bitcast.6, bf16[64,256]{1,0:T(8,128)(2,1)} %bitcast.7, ...), custom_call_target="tpu_custom_call" | custom-call | tf_op jit(solution)/shard_map/pallas_call | solution.py:175
  1.0 3.0 %collective-permute-start = (bf16[64,128]{1,0:T(8,128)(2,1)S(1)}, bf16[64,128]{1,0:T(8,128)(2,1)S(1)}, u32[]{:S(2)}, u32[]{:S(2)}) collective-permute-start(bf16[64,128]{1,0:T(8,128)(2,1)S(1)} %get-tuple-element.19), channel_id=1, source_target_pairs={{2,0},{0,2},{3,1},{1,3},{6,4},{4,6},{7,5},{5,7},{10,8},{8,10},{11,... | collective-permute-start | bytes 49160 | tf_op jit(solution)/shard_map/ppermute | solution.py:228
  4.1 1.5 %shard_map.56 = (bf16[128,896]{1,0:T(8,128)(2,1)S(1)}, bf16[512,640]{1,0:T(8,128)(2,1)S(1)}, s32[8,128]{1,0:T(8,128)S(1)}) custom-call(bf16[64,1024]{1,0:T(8,128)(2,1)S(1)} %get-tuple-element.18.x_ref, s32[64,256]{1,0:T(8,128)S(1)} %get-tuple-element.20.off_ref, bf16[64,256]{1,0:T(8,128)(2,1)S(1)} %get-tuple-element.21.wt_ref, ...), custom_call_target="tpu_custom_call" | custom-call | tf_op jit(solution)/shard_map/pallas_call | solution.py:175
  5.6 0.2 %collective-permute-done.next_ref = bf16[64,128]{1,0:T(8,128)(2,1)S(1)} collective-permute-done((bf16[64,128]{1,0:T(8,128)(2,1)S(1)}, bf16[64,128]{1,0:T(8,128)(2,1)S(1)}, u32[]{:S(2)}, u32[]{:S(2)}) %collective-permute-start) | collective-permute-done | bytes 16416 | tf_op jit(solution)/shard_map/ppermute | solution.py:228
  5.8 0.5 %shard_map.57 = (bf16[32,1024]{1,0:T(8,128)(2,1)S(1)}, bf16[32,1024]{1,0:T(8,128)(2,1)S(1)}, bf16[32,1024]{1,0:T(8,128)(2,1)S(1)}, bf16[32,1024]{1,0:T(8,128)(2,1)S(1)}) custom-call(bf16[64,1024]{1,0:T(8,128)(2,1)S(1)} %get-tuple-element.18.x_ref, bf16[64,128]{1,0:T(8,128)(2,1)S(1)} %collective-permute-done.next_ref, ...), custom_call_target="tpu_custom_call" | custom-call | tf_op jit(solution)/shard_map/pallas_call | solution.py:175
  6.3 2.2 %collective-permute-start.2 = (bf16[32,1024]{1,0:T(8,128)(2,1)S(1)}, bf16[32,1024]{1,0:T(8,128)(2,1)S(1)}, u32[]{:S(2)}, u32[]{:S(2)}) collective-permute-start(bf16[32,1024]{1,0:T(8,128)(2,1)S(1)} %get-tuple-element.30), channel_id=1, source_target_pairs={{0,4},{4,0},{8,12},{12,8},{1,5},{5,1},{9,13},{13,9},{2,6},{6,2},{1... | collective-permute-start | bytes 196616 | tf_op jit(solution)/shard_map/ppermute | solution.py:259
  8.5 0.1 collective-permute-start.1
  8.6 2.5 %collective-permute-done.2.recv_ref = bf16[32,1024]{1,0:T(8,128)(2,1)S(1)} collective-permute-done((bf16[32,1024]{1,0:T(8,128)(2,1)S(1)}, bf16[32,1024]{1,0:T(8,128)(2,1)S(1)}, u32[]{:S(2)}, u32[]{:S(2)}) %collective-permute-start.2) | collective-permute-done | bytes 65568 | tf_op jit(solution)/shard_map/ppermute | solution.py:259
  11.1 2.8 %collective-permute-start.3 = (bf16[32,1024]{1,0:T(8,128)(2,1)S(1)}, bf16[32,1024]{1,0:T(8,128)(2,1)S(1)}, u32[]{:S(2)}, u32[]{:S(2)}) collective-permute-start(bf16[32,1024]{1,0:T(8,128)(2,1)S(1)} %shard_map.59), channel_id=1, source_target_pairs={{0,8},{4,12},{8,0},{12,4},{1,9},{5,13},{9,1},{13,5},{2,10},{6,14},... | collective-permute-start | bytes 196616 | tf_op jit(solution)/shard_map/ppermute | solution.py:265
  13.9 0.0 collective-permute-done.1.recv_ref
  13.9 2.4 %collective-permute-done.3.recv_ref = bf16[32,1024]{1,0:T(8,128)(2,1)S(1)} collective-permute-done((bf16[32,1024]{1,0:T(8,128)(2,1)S(1)}, bf16[32,1024]{1,0:T(8,128)(2,1)S(1)}, u32[]{:S(2)}, u32[]{:S(2)}) %collective-permute-start.3) | collective-permute-done | bytes 65568 | tf_op jit(solution)/shard_map/ppermute | solution.py:265
  16.3 0.6 %shard_map.60 = bf16[32,1024]{1,0:T(8,128)(2,1)} custom-call(bf16[32,1024]{1,0:T(8,128)(2,1)S(1)} %shard_map.58.keep_ref, bf16[32,1024]{1,0:T(8,128)(2,1)S(1)} %collective-permute-done.3.recv_ref), custom_call_target="tpu_custom_call" | custom-call | tf_op jit(solution)/shard_map/pallas_call | solution.py:175
  (2 shorter events, 0.0 us)
Async XLA Ops:
  1.0 4.8 %collective-permute-start = (bf16[64,128]{1,0:T(8,128)(2,1)S(1)}, bf16[64,128]{1,0:T(8,128)(2,1)S(1)}, u32[]{:S(2)}, u32[]{:S(2)}) collective-permute-start(bf16[64,128]{1,0:T(8,128)(2,1)S(1)} %get-tuple-element.19), channel_id=1, source_target_pairs={{2,0},{0,2},{3,1},{1,3},{6,4},{4,6},{7,5},{5,7},{10,8},{8,10},{11,... | collective-permute-start | bytes 49160 | tf_op jit(solution)/shard_map/ppermute | solution.py:228
  6.3 4.7 %collective-permute-start.2 = (bf16[32,1024]{1,0:T(8,128)(2,1)S(1)}, bf16[32,1024]{1,0:T(8,128)(2,1)S(1)}, u32[]{:S(2)}, u32[]{:S(2)}) collective-permute-start(bf16[32,1024]{1,0:T(8,128)(2,1)S(1)} %get-tuple-element.30), channel_id=1, source_target_pairs={{0,4},{4,0},{8,12},{12,8},{1,5},{5,1},{9,13},{13,9},{2,6},{6,2},{1... | collective-permute-start | bytes 196616 | tf_op jit(solution)/shard_map/ppermute | solution.py:259
  8.5 5.4 %collective-permute-start.1 = (bf16[32,1024]{1,0:T(8,128)(2,1)S(1)}, bf16[32,1024]{1,0:T(8,128)(2,1)S(1)}, u32[]{:S(2)}, u32[]{:S(2)}) collective-permute-start(bf16[32,1024]{1,0:T(8,128)(2,1)S(1)} %get-tuple-element.28), channel_id=1, source_target_pairs={{0,4},{4,0},{8,12},{12,8},{1,5},{5,1},{9,13},{13,9},{2,6},{6,2},{1... | collective-permute-start | bytes 196616 | tf_op jit(solution)/shard_map/ppermute | solution.py:260
  11.1 5.2 %collective-permute-start.3 = (bf16[32,1024]{1,0:T(8,128)(2,1)S(1)}, bf16[32,1024]{1,0:T(8,128)(2,1)S(1)}, u32[]{:S(2)}, u32[]{:S(2)}) collective-permute-start(bf16[32,1024]{1,0:T(8,128)(2,1)S(1)} %shard_map.59), channel_id=1, source_target_pairs={{0,8},{4,12},{8,0},{12,4},{1,9},{5,13},{9,1},{13,5},{2,10},{6,14},... | collective-permute-start | bytes 196616 | tf_op jit(solution)/shard_map/ppermute | solution.py:265

commit v4 on v3

--- a/solution.py
+++ b/solution.py
@@ -14,17 +14,11 @@
 PLANES = (MAXOFF - 1 + FINE - 1) // FINE + 1
 
 
-def bit_reversed(count):
-    order = [0]
-    while len(order) < count:
-        order = [2 * r for r in order] + [2 * r + 1 for r in order]
-    return order
-
-
 def own_columns(freq_count, map_ref, del_ref):
     trials = map_ref.shape[1]
-    row_block = trials // (2 * freq_count)
-    rows = trials // 2
+    core_count = lax.axis_size("trial")
+    row_block = trials // (core_count * freq_count)
+    rows = trials // core_count
     levels = freq_count.bit_length() - 1
     freq_index = lax.axis_index("freq")
     core_index = lax.axis_index("trial")
@@ -39,10 +33,11 @@
     )
     place = lax.broadcasted_iota(jnp.int32, (8, rows), 1) // row_block
     mine = jnp.zeros((8, rows), jnp.int32)
-    for position, r in enumerate(bit_reversed(freq_count)):
-        start = ((freq_index ^ r) * 2 + core_index) * row_block
-        turn = lax.rem(position * row_block - start + trials, trials)
-        mine = jnp.where(place == position, pltpu.roll(both, turn, 1)[:, :rows], mine)
+    for r in range(freq_count):
+        core = core_index if r == 0 else core_count - 1 - core_index
+        start = ((freq_index ^ r) * core_count + core) * row_block
+        turn = lax.rem(r * row_block - start + trials, trials)
+        mine = jnp.where(place == r, pltpu.roll(both, turn, 1)[:, :rows], mine)
     return mine
 
 
@@ -157,15 +152,11 @@
     return (a.astype(jnp.float32) + b.astype(jnp.float32)).astype(jnp.bfloat16)
 
 
-def merge_kernel(keep_ref, recv_ref, *outs):
-    piece = outs[0].shape[0]
-    for part, out_ref in enumerate(outs):
-        rows = slice(part * piece, (part + 1) * piece)
-        out_ref[...] = add_bf16(keep_ref[rows, :], recv_ref[rows, :])
-
-
-def final_kernel(keep_ref, recv_ref, out_ref):
-    out_ref[...] = add_bf16(keep_ref[...], recv_ref[...])
+def final_kernel(order, *refs):
+    planes = [refs[order.index(r)][...] for r in range(len(order))]
+    while len(planes) > 1:
+        planes = [add_bf16(lower, upper) for lower, upper in zip(planes[::2], planes[1::2])]
+    refs[-1][...] = planes[0]
 
 
 def call(kernel, outs, *args, scratch=(), limit=16 << 20, space=None):
@@ -191,7 +182,8 @@
     freq_count = lax.axis_size("freq")
     tm_count = lax.axis_size("tm")
     levels = freq_count.bit_length() - 1
-    rows = trials // 2
+    core_count = lax.axis_size("trial")
+    rows = trials // core_count
     span = levels * SHIFT
     tail = -(-(MAXOFF - 1 + span) // LANES) * LANES
     body = seg - tail
@@ -224,8 +216,12 @@
         scratch=(pltpu.SemaphoreType.DMA((6,)),),
         space=pltpu.HBM,
     )
-    ring = [((m + 1) % tm_count, m) for m in range(tm_count)]
-    following = lax.ppermute(edge, "tm", ring)
+    ring = [
+        (((m + 1) % tm_count) * core_count + core_count - 1 - c, m * core_count + c)
+        for m in range(tm_count)
+        for c in range(core_count)
+    ]
+    following = lax.ppermute(edge, ("tm", "trial"), ring)
     planes, taps, columns = call(
         functools.partial(main_kernel, freq_count),
         [
@@ -240,10 +236,9 @@
         lateness,
         scratch=scratch(body),
     )
-    parts = 4 if levels > 1 else 2
-    pieces = call(
-        functools.partial(tail_kernel, freq_count, tm_count, parts),
-        [plane_of(rows // parts, seg)] * parts,
+    blocks = call(
+        functools.partial(tail_kernel, freq_count, tm_count, freq_count),
+        [plane_of(rows // freq_count, seg)] * freq_count,
         samples,
         following,
         taps,
@@ -251,19 +246,16 @@
         planes,
         scratch=scratch(tail),
     )
-    for level in range(levels - 1):
-        swap = [(i, i ^ (1 << level)) for i in range(freq_count)]
-        keep_first, keep_next, send_first, send_next = pieces
-        count = 1 if level == levels - 2 else 2
-        shapes = [plane_of(keep_first.shape[0] // count, seg)] * count
-        early = lax.ppermute(send_next, "freq", swap)
-        late = lax.ppermute(send_first, "freq", swap)
-        forwarded = call(merge_kernel, shapes, keep_next, early)
-        kept = call(merge_kernel, shapes, keep_first, late)
-        pieces = [*kept, *forwarded]
-    keep, send = pieces
-    recv = lax.ppermute(send, "freq", [(i, i ^ (1 << (levels - 1))) for i in range(freq_count)])
-    return call(final_kernel, plane_of(*keep.shape), keep, recv)
+    order = [0, freq_count - 1, *range(1, freq_count - 1)]
+    received = [blocks[0]]
+    for r in order[1:]:
+        route = [
+            (f * core_count + c, (f ^ r) * core_count + core_count - 1 - c)
+            for f in range(freq_count)
+            for c in range(core_count)
+        ]
+        received.append(lax.ppermute(blocks[r], ("freq", "trial"), route))
+    return call(functools.partial(final_kernel, order), plane_of(*blocks[0].shape), *received)
 
 
 def solution(mesh):

time: 17.1 us -> 16.1 us (0.942)
  starting transfers between devices: 8.07 us -> 7.33 us
  waiting for transfers between devices: 5.1 us -> 4.83 us
    ppermute x4, starting transfers between devices: 8.07 us -> 7.33 us  [the longest x3 4.86 us: shards(): received.append(lax.ppermute(blocks[r], ('freq', 'trial'), route))]
    ppermute x4, waiting for transfers between devices: 5.1 us -> 4.83 us  [the longest x3 4.82 us: shards(): received.append(lax.ppermute(blocks[r], ('freq', 'trial'), route))]
    pallas_call x6 -> x4, Pallas kernels: 3.75 us -> 3.74 us  [call(): pl.pallas_call(kernel, out_shape=outs, **specs, scratch_shapes=list(scrat...]
  transfers between devices with their start and end apart: 4 -> 4, of which waited for: 3 -> 2; matrix products, arithmetic and copies ran while one was open for 0% -> 0% of each run, Pallas kernels for 9% -> 9%
where the time goes in v4:
time: 16.1 us; the launch traced here: 15.9 us
  starting transfers between devices  7.33 us (46%)
  waiting for transfers between devices  4.83 us (30%)
  Pallas kernels  3.74 us (23%)
    ppermute x3, starting transfers between devices, shards(): received.append(lax.ppermute(blocks[r], ('freq', 'trial'), route))  4.86 us
    ppermute x3, waiting for transfers between devices, shards(): received.append(lax.ppermute(blocks[r], ('freq', 'trial'), route))  4.82 us
    pallas_call x4, Pallas kernels, call(): pl.pallas_call(kernel, out_shape=outs, **specs, scratch_shapes=list(scrat...  3.74 us
    ppermute x1, starting transfers between devices, shards(): following = lax.ppermute(edge, ('tm', 'trial'), ring)  2.47 us
  transfers between devices with their start and end apart: 4, of which 2 were waited for; matrix products, arithmetic and copies ran while one was open for 0% of the time, Pallas kernels for 9%

profile of v4, /device:TPU:0, one launch (start us, length us, event | category | flops | bytes accessed | tf_op | source)
XLA Modules:
  0.0 15.9 jit_solution(8563803400979335638)
XLA Ops:
  0.0 1.0 %shard_map.55 = (bf16[64,128]{1,0:T(8,128)(2,1)S(1)}, bf16[64,1024]{1,0:T(8,128)(2,1)S(1)}, s32[64,256]{1,0:T(8,128)S(1)}, bf16[64,256]{1,0:T(8,128)(2,1)S(1)}, ...) custom-call(bf16[64,1024]{1,0:T(8,128)(2,1)} %x_hbm.1, s32[64,256]{1,0:T(8,128)} %bitcast.6, bf16[64,256]{1,0:T(8,128)(2,1)} %bitcast.7, ...), custom_call_target="tpu_custom_call" | custom-call | tf_op jit(solution)/shard_map/pallas_call | solution.py:166
  1.0 2.5 %collective-permute-start = (bf16[64,128]{1,0:T(8,128)(2,1)S(1)}, bf16[64,128]{1,0:T(8,128)(2,1)S(1)}, u32[]{:S(2)}, u32[]{:S(2)}) collective-permute-start(bf16[64,128]{1,0:T(8,128)(2,1)S(1)} %get-tuple-element.19), channel_id=1, source_target_pairs={{3,0},{2,1},{1,2},{0,3},{7,4},{6,5},{5,6},{4,7},{11,8},{10,9},{9,1... | collective-permute-start | bytes 49160 | tf_op jit(solution)/shard_map/ppermute | solution.py:224
  3.5 1.5 %shard_map.56 = (bf16[128,896]{1,0:T(8,128)(2,1)S(1)}, bf16[512,640]{1,0:T(8,128)(2,1)S(1)}, s32[8,128]{1,0:T(8,128)S(1)}) custom-call(bf16[64,1024]{1,0:T(8,128)(2,1)S(1)} %get-tuple-element.18.x_ref, s32[64,256]{1,0:T(8,128)S(1)} %get-tuple-element.20.off_ref, bf16[64,256]{1,0:T(8,128)(2,1)S(1)} %get-tuple-element.21.wt_ref, ...), custom_call_target="tpu_custom_call" | custom-call | tf_op jit(solution)/shard_map/pallas_call | solution.py:166
  5.0 0.0 collective-permute-done.next_ref
  5.0 0.5 %shard_map.57 = (bf16[32,1024]{1,0:T(8,128)(2,1)S(1)}, bf16[32,1024]{1,0:T(8,128)(2,1)S(1)}, bf16[32,1024]{1,0:T(8,128)(2,1)S(1)}, bf16[32,1024]{1,0:T(8,128)(2,1)S(1)}) custom-call(bf16[64,1024]{1,0:T(8,128)(2,1)S(1)} %get-tuple-element.18.x_ref, bf16[64,128]{1,0:T(8,128)(2,1)S(1)} %collective-permute-done.next_ref, ...), custom_call_target="tpu_custom_call" | custom-call | tf_op jit(solution)/shard_map/pallas_call | solution.py:166
  5.6 4.2 %collective-permute-start.1 = (bf16[32,1024]{1,0:T(8,128)(2,1)S(1)}, bf16[32,1024]{1,0:T(8,128)(2,1)S(1)}, u32[]{:S(2)}, u32[]{:S(2)}) collective-permute-start(bf16[32,1024]{1,0:T(8,128)(2,1)S(1)} %get-tuple-element.28), channel_id=1, source_target_pairs={{0,13},{1,12},{4,9},{5,8},{8,5},{9,4},{12,1},{13,0},{2,15},{3,14},... | collective-permute-start | bytes 196616 | tf_op jit(solution)/shard_map/ppermute | solution.py:257
  9.8 0.0 collective-permute-start.2
  9.8 0.6 %collective-permute-start.3 = (bf16[32,1024]{1,0:T(8,128)(2,1)S(1)}, bf16[32,1024]{1,0:T(8,128)(2,1)S(1)}, u32[]{:S(2)}, u32[]{:S(2)}) collective-permute-start(bf16[32,1024]{1,0:T(8,128)(2,1)S(1)} %get-tuple-element.30), channel_id=1, source_target_pairs={{0,9},{1,8},{4,13},{5,12},{8,1},{9,0},{12,5},{13,4},{2,11},{3,10},... | collective-permute-start | bytes 196616 | tf_op jit(solution)/shard_map/ppermute | solution.py:257
  10.4 1.8 %collective-permute-done.1.refs_1_ = bf16[32,1024]{1,0:T(8,128)(2,1)S(1)} collective-permute-done((bf16[32,1024]{1,0:T(8,128)(2,1)S(1)}, bf16[32,1024]{1,0:T(8,128)(2,1)S(1)}, u32[]{:S(2)}, u32[]{:S(2)}) %collective-permute-start.1) | collective-permute-done | bytes 65568 | tf_op jit(solution)/shard_map/ppermute | solution.py:257
  12.3 3.0 %collective-permute-done.2.refs_2_ = bf16[32,1024]{1,0:T(8,128)(2,1)S(1)} collective-permute-done((bf16[32,1024]{1,0:T(8,128)(2,1)S(1)}, bf16[32,1024]{1,0:T(8,128)(2,1)S(1)}, u32[]{:S(2)}, u32[]{:S(2)}) %collective-permute-start.2) | collective-permute-done | bytes 65568 | tf_op jit(solution)/shard_map/ppermute | solution.py:257
  15.3 0.0 collective-permute-done.3.refs_3_
  15.3 0.7 %shard_map.58 = bf16[32,1024]{1,0:T(8,128)(2,1)} custom-call(bf16[32,1024]{1,0:T(8,128)(2,1)S(1)} %get-tuple-element.27.refs_0_, bf16[32,1024]{1,0:T(8,128)(2,1)S(1)} %collective-permute-done.1.refs_1_, bf16[32,1024]{1,0:T(8,128)(2,1)S(1)} %collective-permute-done.2.refs_2_, bf16[32,1024]{1,0:T(8,128)(2,1)S(1)} %collective-permute-done.3.refs_3_), custom_call_target="tpu_custom_call" | custom-call | tf_op jit(solution)/shard_map/pallas_call | solution.py:166
Async XLA Ops:
  1.0 4.0 %collective-permute-start = (bf16[64,128]{1,0:T(8,128)(2,1)S(1)}, bf16[64,128]{1,0:T(8,128)(2,1)S(1)}, u32[]{:S(2)}, u32[]{:S(2)}) collective-permute-start(bf16[64,128]{1,0:T(8,128)(2,1)S(1)} %get-tuple-element.19), channel_id=1, source_target_pairs={{3,0},{2,1},{1,2},{0,3},{7,4},{6,5},{5,6},{4,7},{11,8},{10,9},{9,1... | collective-permute-start | bytes 49160 | tf_op jit(solution)/shard_map/ppermute | solution.py:224
  5.6 6.7 %collective-permute-start.1 = (bf16[32,1024]{1,0:T(8,128)(2,1)S(1)}, bf16[32,1024]{1,0:T(8,128)(2,1)S(1)}, u32[]{:S(2)}, u32[]{:S(2)}) collective-permute-start(bf16[32,1024]{1,0:T(8,128)(2,1)S(1)} %get-tuple-element.28), channel_id=1, source_target_pairs={{0,13},{1,12},{4,9},{5,8},{8,5},{9,4},{12,1},{13,0},{2,15},{3,14},... | collective-permute-start | bytes 196616 | tf_op jit(solution)/shard_map/ppermute | solution.py:257
  9.8 5.5 %collective-permute-start.2 = (bf16[32,1024]{1,0:T(8,128)(2,1)S(1)}, bf16[32,1024]{1,0:T(8,128)(2,1)S(1)}, u32[]{:S(2)}, u32[]{:S(2)}) collective-permute-start(bf16[32,1024]{1,0:T(8,128)(2,1)S(1)} %get-tuple-element.29), channel_id=1, source_target_pairs={{0,5},{1,4},{4,1},{5,0},{8,13},{9,12},{12,9},{13,8},{2,7},{3,6},{6... | collective-permute-start | bytes 196616 | tf_op jit(solution)/shard_map/ppermute | solution.py:257
  9.8 5.5 %collective-permute-start.3 = (bf16[32,1024]{1,0:T(8,128)(2,1)S(1)}, bf16[32,1024]{1,0:T(8,128)(2,1)S(1)}, u32[]{:S(2)}, u32[]{:S(2)}) collective-permute-start(bf16[32,1024]{1,0:T(8,128)(2,1)S(1)} %get-tuple-element.30), channel_id=1, source_target_pairs={{0,9},{1,8},{4,13},{5,12},{8,1},{9,0},{12,5},{13,4},{2,11},{3,10},... | collective-permute-start | bytes 196616 | tf_op jit(solution)/shard_map/ppermute | solution.py:257

commit v5 on v4

--- a/solution.py
+++ b/solution.py
@@ -12,6 +12,19 @@
 LANES = 128
 FINE = 8
 PLANES = (MAXOFF - 1 + FINE - 1) // FINE + 1
+
+
+def shared_pairs(freq_count):
+    return [(r, r + 1) for r in range(1, freq_count - 1, 2)]
+
+
+def block_order(freq_count, core_index):
+    other = 1 - core_index
+    order = [(0, core_index)]
+    for first, second in shared_pairs(freq_count):
+        mine = first + core_index * (second - first)
+        order += [(mine, core_index), (mine, other)]
+    return [*order, (freq_count - 1, other)]
 
 
 def own_columns(freq_count, map_ref, del_ref):
@@ -33,11 +46,10 @@
     )
     place = lax.broadcasted_iota(jnp.int32, (8, rows), 1) // row_block
     mine = jnp.zeros((8, rows), jnp.int32)
-    for r in range(freq_count):
-        core = core_index if r == 0 else core_count - 1 - core_index
-        start = ((freq_index ^ r) * core_count + core) * row_block
-        turn = lax.rem(r * row_block - start + trials, trials)
-        mine = jnp.where(place == r, pltpu.roll(both, turn, 1)[:, :rows], mine)
+    for position, (distance, core) in enumerate(block_order(freq_count, core_index)):
+        start = ((freq_index ^ distance) * core_count + core) * row_block
+        turn = lax.rem(position * row_block - start + trials, trials)
+        mine = jnp.where(place == position, pltpu.roll(both, turn, 1)[:, :rows], mine)
     return mine
 
 
@@ -130,33 +142,43 @@
 
 
 def tail_kernel(
-    freq_count, tm_count, parts, x_ref, next_ref, rhs_ref, delay_ref, body_ref, *rest
+    freq_count, tm_count, x_ref, next_ref, rhs_ref, delay_ref, body_ref, *rest
 ):
-    outs, (time_ref, lhs_ref, plane_ref, leaf_ref) = rest[:parts], rest[parts:]
+    outs, (time_ref, lhs_ref, plane_ref, leaf_ref) = rest[:-4], rest[-4:]
     body = body_ref.shape[1]
     tail = x_ref.shape[1] - body
-    piece = outs[0].shape[0]
     span = (freq_count.bit_length() - 1) * SHIFT
     inside = lax.axis_index("tm") < tm_count - 1
     following = jnp.where(inside, next_ref[...].astype(jnp.float32), 0.0).astype(jnp.bfloat16)
     window = jnp.concatenate([x_ref[:, body:], following], axis=1)
     blocks = convolve(window, span, tail, delay_ref[1:2, :], rhs_ref, time_ref, lhs_ref, plane_ref, leaf_ref)
-    for part, out_ref in enumerate(outs):
-        rows = slice(part * piece, (part + 1) * piece)
+    first = 0
+    for out_ref in outs:
+        rows = slice(first, first + out_ref.shape[0])
+        first += out_ref.shape[0]
         out_ref[:, :body] = body_ref[rows, :]
         for index, block in enumerate(blocks):
             out_ref[:, body + index * LANES : body + (index + 1) * LANES] = block[rows]
 
 
-def add_bf16(a, b):
-    return (a.astype(jnp.float32) + b.astype(jnp.float32)).astype(jnp.bfloat16)
-
-
-def final_kernel(order, *refs):
-    planes = [refs[order.index(r)][...] for r in range(len(order))]
+def second_half_kernel(both_ref, out_ref):
+    out_ref[...] = both_ref[out_ref.shape[0] :, :]
+
+
+def final_kernel(freq_count, own_ref, *refs):
+    piece = own_ref.shape[0]
+    first_core = lax.axis_index("trial") == 0
+    planes = [own_ref[...].astype(jnp.float32)]
+    for pair in range(len(shared_pairs(freq_count))):
+        here = refs[2 * pair][:piece, :].astype(jnp.float32)
+        there = refs[2 * pair + 1][...].astype(jnp.float32)
+        planes += [jnp.where(first_core, here, there), jnp.where(first_core, there, here)]
+    planes.append(refs[-2][...].astype(jnp.float32))
     while len(planes) > 1:
-        planes = [add_bf16(lower, upper) for lower, upper in zip(planes[::2], planes[1::2])]
-    refs[-1][...] = planes[0]
+        planes = [
+            (lower + upper).astype(jnp.bfloat16).astype(jnp.float32) for lower, upper in zip(planes[::2], planes[1::2])
+        ]
+    refs[-1][...] = planes[0].astype(jnp.bfloat16)
 
 
 def call(kernel, outs, *args, scratch=(), limit=16 << 20, space=None):
@@ -236,9 +258,11 @@
         lateness,
         scratch=scratch(body),
     )
-    blocks = call(
-        functools.partial(tail_kernel, freq_count, tm_count, freq_count),
-        [plane_of(rows // freq_count, seg)] * freq_count,
+    piece = rows // freq_count
+    pairs = shared_pairs(freq_count)
+    own, *shared, far = call(
+        functools.partial(tail_kernel, freq_count, tm_count),
+        [plane_of(piece, seg), *[plane_of(2 * piece, seg)] * len(pairs), plane_of(piece, seg)],
         samples,
         following,
         taps,
@@ -246,16 +270,18 @@
         planes,
         scratch=scratch(tail),
     )
-    order = [0, freq_count - 1, *range(1, freq_count - 1)]
-    received = [blocks[0]]
-    for r in order[1:]:
-        route = [
-            (f * core_count + c, (f ^ r) * core_count + core_count - 1 - c)
-            for f in range(freq_count)
-            for c in range(core_count)
-        ]
-        received.append(lax.ppermute(blocks[r], ("freq", "trial"), route))
-    return call(functools.partial(final_kernel, order), plane_of(*blocks[0].shape), *received)
+    devices = [(f, c) for f in range(freq_count) for c in range(core_count)]
+    arrived = []
+    for pair, block in zip(pairs, shared):
+        route = [(f * core_count + c, (f ^ pair[c]) * core_count + c) for f, c in devices]
+        arrived.append(lax.ppermute(block, ("freq", "trial"), route))
+    route = [(f * core_count + c, (f ^ (freq_count - 1)) * core_count + core_count - 1 - c) for f, c in devices]
+    far = lax.ppermute(far, ("freq", "trial"), route)
+    received = []
+    for both in arrived:
+        handed = call(second_half_kernel, plane_of(piece, seg), both)
+        received += [both, lax.ppermute(handed, "trial", [(0, 1), (1, 0)])]
+    return call(functools.partial(final_kernel, freq_count), plane_of(piece, seg), own, *received, far)
 
 
 def solution(mesh):

time: 16.1 us -> 15.5 us (0.963)
  the two profiles are of different devices: /device:TPU:0 before, /device:TPU:1 now
where the time goes in v5:
time: 15.5 us; the launch traced here: 15.4 us
  starting transfers between devices  7.06 us (46%)
  waiting for transfers between devices  4.5 us (29%)
  Pallas kernels  3.77 us (24%)
    pallas_call x5, Pallas kernels, call(): pl.pallas_call(kernel, out_shape=outs, **specs, scratch_shapes=list(scrat...  3.77 us
    ppermute x1, starting transfers between devices, shards(): following = lax.ppermute(edge, ('tm', 'trial'), ring)  2.65 us
    ppermute x1, starting transfers between devices, shards(): arrived.append(lax.ppermute(block, ('freq', 'trial'), route))  2.65 us
    ppermute x1, waiting for transfers between devices, shards(): far = lax.ppermute(far, ('freq', 'trial'), route)  2.53 us
    ppermute x1, waiting for transfers between devices, shards(): arrived.append(lax.ppermute(block, ('freq', 'trial'), route))  1.97 us
    ppermute x1, starting transfers between devices, shards(): far = lax.ppermute(far, ('freq', 'trial'), route)  1.74 us
  transfers between devices with their start and end apart: 4, of which 2 were waited for; matrix products, arithmetic and copies ran while one was open for 0% of the time, Pallas kernels for 10%

profile of v5, /device:TPU:1, one launch (start us, length us, event | category | flops | bytes accessed | tf_op | source)
XLA Modules:
  0.0 15.4 jit_solution(12652034034890346554)
XLA Ops:
  0.0 1.0 %shard_map.55 = (bf16[64,128]{1,0:T(8,128)(2,1)S(1)}, bf16[64,1024]{1,0:T(8,128)(2,1)S(1)}, s32[64,256]{1,0:T(8,128)S(1)}, bf16[64,256]{1,0:T(8,128)(2,1)S(1)}, ...) custom-call(bf16[64,1024]{1,0:T(8,128)(2,1)} %x_hbm.1, s32[64,256]{1,0:T(8,128)} %bitcast.6, bf16[64,256]{1,0:T(8,128)(2,1)} %bitcast.7, ...), custom_call_target="tpu_custom_call" | custom-call | tf_op jit(solution)/shard_map/pallas_call | solution.py:188
  1.0 2.7 %collective-permute-start = (bf16[64,128]{1,0:T(8,128)(2,1)S(1)}, bf16[64,128]{1,0:T(8,128)(2,1)S(1)}, u32[]{:S(2)}, u32[]{:S(2)}) collective-permute-start(bf16[64,128]{1,0:T(8,128)(2,1)S(1)} %get-tuple-element.18), channel_id=1, source_target_pairs={{3,0},{2,1},{1,2},{0,3},{7,4},{6,5},{5,6},{4,7},{11,8},{10,9},{9,1... | collective-permute-start | bytes 49160 | tf_op jit(solution)/shard_map/ppermute | solution.py:246
  3.7 1.5 %shard_map.56 = (bf16[128,896]{1,0:T(8,128)(2,1)S(1)}, bf16[512,640]{1,0:T(8,128)(2,1)S(1)}, s32[8,128]{1,0:T(8,128)S(1)}) custom-call(bf16[64,1024]{1,0:T(8,128)(2,1)S(1)} %get-tuple-element.17.x_ref, s32[64,256]{1,0:T(8,128)S(1)} %get-tuple-element.19.off_ref, bf16[64,256]{1,0:T(8,128)(2,1)S(1)} %get-tuple-element.20.wt_ref, ...), custom_call_target="tpu_custom_call" | custom-call | tf_op jit(solution)/shard_map/pallas_call | solution.py:188
  5.2 0.0 collective-permute-done.next_ref
  5.2 0.5 %shard_map.57 = (bf16[32,1024]{1,0:T(8,128)(2,1)S(1)}, bf16[64,1024]{1,0:T(8,128)(2,1)S(1)}, bf16[32,1024]{1,0:T(8,128)(2,1)S(1)}) custom-call(bf16[64,1024]{1,0:T(8,128)(2,1)S(1)} %get-tuple-element.17.x_ref, bf16[64,128]{1,0:T(8,128)(2,1)S(1)} %collective-permute-done.next_ref, bf16[512,640]{1,0:T(8,128)(2,1)S(1)} %get-tuple-element.23.rhs_ref, ...), custom_call_target="tpu_custom_call" | custom-call | tf_op jit(solution)/shard_map/pallas_call | solution.py:188
  5.8 2.6 %collective-permute-start.1 = (bf16[64,1024]{1,0:T(8,128)(2,1)S(1)}, bf16[64,1024]{1,0:T(8,128)(2,1)S(1)}, u32[]{:S(2)}, u32[]{:S(2)}) collective-permute-start(bf16[64,1024]{1,0:T(8,128)(2,1)S(1)} %get-tuple-element.27), channel_id=1, source_target_pairs={{0,4},{1,9},{4,0},{5,13},{8,12},{9,1},{12,8},{13,5},{2,6},{3,11},{... | collective-permute-start | bytes 393224 | tf_op jit(solution)/shard_map/ppermute | solution.py:277
  8.4 1.7 %collective-permute-start.3 = (bf16[32,1024]{1,0:T(8,128)(2,1)S(1)}, bf16[32,1024]{1,0:T(8,128)(2,1)S(1)}, u32[]{:S(2)}, u32[]{:S(2)}) collective-permute-start(bf16[32,1024]{1,0:T(8,128)(2,1)S(1)} %get-tuple-element.28), channel_id=1, source_target_pairs={{0,13},{1,12},{4,9},{5,8},{8,5},{9,4},{12,1},{13,0},{2,15},{3,14},... | collective-permute-start | bytes 196616 | tf_op jit(solution)/shard_map/ppermute | solution.py:279
  10.1 2.0 %collective-permute-done.1.both_ref.refs_0_ = bf16[64,1024]{1,0:T(8,128)(2,1)S(1)} collective-permute-done((bf16[64,1024]{1,0:T(8,128)(2,1)S(1)}, bf16[64,1024]{1,0:T(8,128)(2,1)S(1)}, u32[]{:S(2)}, u32[]{:S(2)}) %collective-permute-start.1) | collective-permute-done | bytes 131104 | tf_op jit(solution)/shard_map/ppermute | solution.py:277
  12.1 0.0 collective-permute-start.2
  12.1 2.5 %collective-permute-done.3.refs_2_ = bf16[32,1024]{1,0:T(8,128)(2,1)S(1)} collective-permute-done((bf16[32,1024]{1,0:T(8,128)(2,1)S(1)}, bf16[32,1024]{1,0:T(8,128)(2,1)S(1)}, u32[]{:S(2)}, u32[]{:S(2)}) %collective-permute-start.3) | collective-permute-done | bytes 65568 | tf_op jit(solution)/shard_map/ppermute | solution.py:279
  14.7 0.0 collective-permute-done.2.refs_1_
  14.7 0.7 %shard_map.59 = bf16[32,1024]{1,0:T(8,128)(2,1)} custom-call(bf16[32,1024]{1,0:T(8,128)(2,1)S(1)} %get-tuple-element.26.own_ref, bf16[64,1024]{1,0:T(8,128)(2,1)S(1)} %collective-permute-done.1.both_ref.refs_0_, bf16[32,1024]{1,0:T(8,128)(2,1)S(1)} %collective-permute-done.2.refs_1_, bf16[32,1024]{1,0:T(8,128)(2,1)S(1)} %collective-permute-done.3.refs_2_), custom_call_target="tpu_custom_call" | custom-call | tf_op jit(solution)/shard_map/pallas_call | solution.py:188
  (1 shorter events, 0.0 us)
Async XLA Ops:
  1.0 4.2 %collective-permute-start = (bf16[64,128]{1,0:T(8,128)(2,1)S(1)}, bf16[64,128]{1,0:T(8,128)(2,1)S(1)}, u32[]{:S(2)}, u32[]{:S(2)}) collective-permute-start(bf16[64,128]{1,0:T(8,128)(2,1)S(1)} %get-tuple-element.18), channel_id=1, source_target_pairs={{3,0},{2,1},{1,2},{0,3},{7,4},{6,5},{5,6},{4,7},{11,8},{10,9},{9,1... | collective-permute-start | bytes 49160 | tf_op jit(solution)/shard_map/ppermute | solution.py:246
  5.8 6.4 %collective-permute-start.1 = (bf16[64,1024]{1,0:T(8,128)(2,1)S(1)}, bf16[64,1024]{1,0:T(8,128)(2,1)S(1)}, u32[]{:S(2)}, u32[]{:S(2)}) collective-permute-start(bf16[64,1024]{1,0:T(8,128)(2,1)S(1)} %get-tuple-element.27), channel_id=1, source_target_pairs={{0,4},{1,9},{4,0},{5,13},{8,12},{9,1},{12,8},{13,5},{2,6},{3,11},{... | collective-permute-start | bytes 393224 | tf_op jit(solution)/shard_map/ppermute | solution.py:277
  8.4 6.3 %collective-permute-start.3 = (bf16[32,1024]{1,0:T(8,128)(2,1)S(1)}, bf16[32,1024]{1,0:T(8,128)(2,1)S(1)}, u32[]{:S(2)}, u32[]{:S(2)}) collective-permute-start(bf16[32,1024]{1,0:T(8,128)(2,1)S(1)} %get-tuple-element.28), channel_id=1, source_target_pairs={{0,13},{1,12},{4,9},{5,8},{8,5},{9,4},{12,1},{13,0},{2,15},{3,14},... | collective-permute-start | bytes 196616 | tf_op jit(solution)/shard_map/ppermute | solution.py:279
  12.1 2.6 %collective-permute-start.2 = (bf16[32,1024]{1,0:T(8,128)(2,1)S(1)}, bf16[32,1024]{1,0:T(8,128)(2,1)S(1)}, u32[]{:S(2)}, u32[]{:S(2)}) collective-permute-start(bf16[32,1024]{1,0:T(8,128)(2,1)S(1)} %shard_map.58), channel_id=1, source_target_pairs={{0,1},{1,0},{2,3},{3,2},{4,5},{5,4},{6,7},{7,6},{8,9},{9,8},{10,11... | collective-permute-start | bytes 196616 | tf_op jit(solution)/shard_map/ppermute | solution.py:283

commit v6 on v5

--- a/solution.py
+++ b/solution.py
@@ -6,6 +6,7 @@
 from jax.experimental import pallas as pl
 from jax.experimental.pallas import tpu as pltpu
 from jax.sharding import PartitionSpec as P
+
 
 MAXOFF = 32
 SHIFT = 32
@@ -107,12 +108,20 @@
     return blocks
 
 
+def store_rows(blocks, outs):
+    first = 0
+    for out_ref in outs:
+        rows = slice(first, first + out_ref.shape[0])
+        first += out_ref.shape[0]
+        for index, block in enumerate(blocks):
+            out_ref[:, index * LANES : (index + 1) * LANES] = block[rows]
+
+
 def load_kernel(x_hbm, off_hbm, wt_hbm, map_hbm, del_hbm, edge_ref, x_ref, off_ref, wt_ref, map_ref, del_ref, sems):
     moves = [
         pltpu.make_async_copy(source, target, sems.at[index])
         for index, (source, target) in enumerate(
             (
-                (x_hbm.at[:, : edge_ref.shape[1]], edge_ref),
                 (x_hbm, x_ref),
                 (off_hbm, off_ref),
                 (wt_hbm, wt_ref),
@@ -123,62 +132,63 @@
     ]
     for move in moves:
         move.start()
-    for move in moves:
+    moves[0].wait()
+    edge_ref[...] = x_ref[:, : edge_ref.shape[1]]
+    for move in moves[1:]:
         move.wait()
 
 
 def main_kernel(
-    freq_count, x_ref, off_ref, wt_ref, map_ref, del_ref,
-    body_ref, rhs_ref, delay_ref, time_ref, lhs_ref, plane_ref, leaf_ref,
+    freq_count, x_ref, off_ref, wt_ref, map_ref, del_ref, rhs_ref, delay_ref, *rest
 ):
+    outs, (time_ref, lhs_ref, plane_ref, leaf_ref) = rest[:-4], rest[-4:]
     mine = own_columns(freq_count, map_ref, del_ref)
     build_taps(off_ref, wt_ref, mine, rhs_ref)
     delay_ref[...] = mine
-    columns = body_ref.shape[1]
+    columns = outs[0].shape[1]
     span = (freq_count.bit_length() - 1) * SHIFT
     blocks = convolve(x_ref[...], span, columns, mine[1:2, :], rhs_ref, time_ref, lhs_ref, plane_ref, leaf_ref)
-    for index, block in enumerate(blocks):
-        body_ref[:, index * LANES : (index + 1) * LANES] = block
-
-
-def tail_kernel(
-    freq_count, tm_count, x_ref, next_ref, rhs_ref, delay_ref, body_ref, *rest
-):
-    outs, (time_ref, lhs_ref, plane_ref, leaf_ref) = rest[:-4], rest[-4:]
-    body = body_ref.shape[1]
-    tail = x_ref.shape[1] - body
+    store_rows(blocks, outs)
+
+
+def tail_kernel(freq_count, tm_count, x_ref, next_ref, rhs_ref, delay_ref, far_body_ref, *rest):
+    outs, far_ref, (time_ref, lhs_ref, plane_ref, leaf_ref) = rest[:-5], rest[-5], rest[-4:]
+    tail = outs[0].shape[1]
+    body = x_ref.shape[1] - tail
     span = (freq_count.bit_length() - 1) * SHIFT
     inside = lax.axis_index("tm") < tm_count - 1
     following = jnp.where(inside, next_ref[...].astype(jnp.float32), 0.0).astype(jnp.bfloat16)
     window = jnp.concatenate([x_ref[:, body:], following], axis=1)
     blocks = convolve(window, span, tail, delay_ref[1:2, :], rhs_ref, time_ref, lhs_ref, plane_ref, leaf_ref)
-    first = 0
-    for out_ref in outs:
-        rows = slice(first, first + out_ref.shape[0])
-        first += out_ref.shape[0]
-        out_ref[:, :body] = body_ref[rows, :]
-        for index, block in enumerate(blocks):
-            out_ref[:, body + index * LANES : body + (index + 1) * LANES] = block[rows]
-
-
-def second_half_kernel(both_ref, out_ref):
-    out_ref[...] = both_ref[out_ref.shape[0] :, :]
-
-
-def final_kernel(freq_count, own_ref, *refs):
-    piece = own_ref.shape[0]
+    far_ref[:, :body] = far_body_ref[...]
+    store_rows(blocks, [*outs, far_ref.at[:, body:]])
+
+
+def second_half_kernel(body_ref, tail_ref, out_ref):
+    piece, _ = out_ref.shape
+    body = body_ref.shape[1]
+    out_ref[:, :body] = body_ref[piece:, :]
+    out_ref[:, body:] = tail_ref[piece:, :]
+
+
+def final_kernel(freq_count, *refs):
+    out_ref = refs[-1]
+    piece, seg = out_ref.shape
+    body = refs[0].shape[1]
     first_core = lax.axis_index("trial") == 0
-    planes = [own_ref[...].astype(jnp.float32)]
-    for pair in range(len(shared_pairs(freq_count))):
-        here = refs[2 * pair][:piece, :].astype(jnp.float32)
-        there = refs[2 * pair + 1][...].astype(jnp.float32)
-        planes += [jnp.where(first_core, here, there), jnp.where(first_core, there, here)]
-    planes.append(refs[-2][...].astype(jnp.float32))
-    while len(planes) > 1:
-        planes = [
-            (lower + upper).astype(jnp.bfloat16).astype(jnp.float32) for lower, upper in zip(planes[::2], planes[1::2])
-        ]
-    refs[-1][...] = planes[0].astype(jnp.bfloat16)
+    for part, columns in ((0, slice(0, body)), (1, slice(body, seg))):
+        planes = [refs[part][...].astype(jnp.float32)]
+        for pair in range(len(shared_pairs(freq_count))):
+            here = refs[2 + 3 * pair + part][:piece, :].astype(jnp.float32)
+            there = refs[2 + 3 * pair + 2][:, columns].astype(jnp.float32)
+            planes += [jnp.where(first_core, here, there), jnp.where(first_core, there, here)]
+        planes.append(refs[-2][:, columns].astype(jnp.float32))
+        while len(planes) > 1:
+            planes = [
+                (lower + upper).astype(jnp.bfloat16).astype(jnp.float32)
+                for lower, upper in zip(planes[::2], planes[1::2])
+            ]
+        out_ref[:, columns] = planes[0].astype(jnp.bfloat16)
 
 
 def call(kernel, outs, *args, scratch=(), limit=16 << 20, space=None):
@@ -235,7 +245,7 @@
         jnp.swapaxes(tap_weights[0], 0, 1),
         trial_map,
         delays,
-        scratch=(pltpu.SemaphoreType.DMA((6,)),),
+        scratch=(pltpu.SemaphoreType.DMA((5,)),),
         space=pltpu.HBM,
     )
     ring = [
@@ -244,12 +254,15 @@
         for c in range(core_count)
     ]
     following = lax.ppermute(edge, ("tm", "trial"), ring)
-    planes, taps, columns = call(
+    piece = rows // freq_count
+    pairs = shared_pairs(freq_count)
+    heights = [piece, *[2 * piece] * len(pairs), piece]
+    taps, columns, *bodies = call(
         functools.partial(main_kernel, freq_count),
         [
-            plane_of(rows, body),
             plane_of(FINE * band, PLANES * rows),
             jax.ShapeDtypeStruct((8, rows), jnp.int32),
+            *[plane_of(height, body) for height in heights],
         ],
         samples,
         lags,
@@ -258,30 +271,35 @@
         lateness,
         scratch=scratch(body),
     )
-    piece = rows // freq_count
-    pairs = shared_pairs(freq_count)
-    own, *shared, far = call(
+    devices = [(f, c) for f in range(freq_count) for c in range(core_count)]
+
+    def traded(blocks):
+        arrived = []
+        for pair, block in zip(pairs, blocks):
+            route = [(f * core_count + c, (f ^ pair[c]) * core_count + c) for f, c in devices]
+            arrived.append(lax.ppermute(block, ("freq", "trial"), route))
+        return arrived
+
+    own, *bodies, far_body = bodies
+    bodies = traded(bodies)
+    own_tail, *tails, far = call(
         functools.partial(tail_kernel, freq_count, tm_count),
-        [plane_of(piece, seg), *[plane_of(2 * piece, seg)] * len(pairs), plane_of(piece, seg)],
+        [*[plane_of(height, tail) for height in heights[:-1]], plane_of(piece, seg)],
         samples,
         following,
         taps,
         columns,
-        planes,
+        far_body,
         scratch=scratch(tail),
     )
-    devices = [(f, c) for f in range(freq_count) for c in range(core_count)]
-    arrived = []
-    for pair, block in zip(pairs, shared):
-        route = [(f * core_count + c, (f ^ pair[c]) * core_count + c) for f, c in devices]
-        arrived.append(lax.ppermute(block, ("freq", "trial"), route))
+    tails = traded(tails)
     route = [(f * core_count + c, (f ^ (freq_count - 1)) * core_count + core_count - 1 - c) for f, c in devices]
     far = lax.ppermute(far, ("freq", "trial"), route)
     received = []
-    for both in arrived:
-        handed = call(second_half_kernel, plane_of(piece, seg), both)
-        received += [both, lax.ppermute(handed, "trial", [(0, 1), (1, 0)])]
-    return call(functools.partial(final_kernel, freq_count), plane_of(piece, seg), own, *received, far)
+    for both in zip(bodies, tails):
+        handed = call(second_half_kernel, plane_of(piece, seg), *both)
+        received += [*both, lax.ppermute(handed, "trial", [(0, 1), (1, 0)])]
+    return call(functools.partial(final_kernel, freq_count), plane_of(piece, seg), own, own_tail, *received, far)
 
 
 def solution(mesh):

time: 15.5 us -> 17.8 us (1.15)
  waiting for transfers between devices: 4.5 us -> 5.77 us
  starting transfers between devices: 7.06 us -> 8.12 us
    ppermute x2 -> x3, starting transfers between devices: 2.67 us -> 5.34 us  [the longest x2 4.97 us: traded(): arrived.append(lax.ppermute(block, ('freq', 'trial'), route))]
    ppermute x1, waiting for transfers between devices: 0.01 us -> 2.4 us  [shards(): following = lax.ppermute(edge, ('tm', 'trial'), ring)]
    ppermute x2 -> x3, waiting for transfers between devices: 1.97 us -> 0.04 us  [the longest x2 0.04 us: traded(): arrived.append(lax.ppermute(block, ('freq', 'trial'), route))]
    ppermute x1, starting transfers between devices: 2.65 us -> 1.04 us  [shards(): following = lax.ppermute(edge, ('tm', 'trial'), ring)]
    ppermute x1, waiting for transfers between devices: 2.53 us -> 3.33 us  [shards(): far = lax.ppermute(far, ('freq', 'trial'), route)]
  transfers between devices with their start and end apart: 4 -> 5, of which waited for: 2 -> 2; matrix products, arithmetic and copies ran while one was open for 0% -> 0% of each run, Pallas kernels for 10% -> 3%
where the time goes in v6:
time: 17.8 us; the launch traced here: 17.6 us
  starting transfers between devices  8.12 us (46%)
  waiting for transfers between devices  5.77 us (32%)
  Pallas kernels  3.7 us (21%)
    ppermute x2, starting transfers between devices, traded(): arrived.append(lax.ppermute(block, ('freq', 'trial'), route))  4.97 us
    pallas_call x5, Pallas kernels, call(): pl.pallas_call(kernel, out_shape=outs, **specs, scratch_shapes=list(scrat...  3.7 us
    ppermute x1, waiting for transfers between devices, shards(): far = lax.ppermute(far, ('freq', 'trial'), route)  3.33 us
    ppermute x1, waiting for transfers between devices, shards(): following = lax.ppermute(edge, ('tm', 'trial'), ring)  2.4 us
    ppermute x1, starting transfers between devices, shards(): far = lax.ppermute(far, ('freq', 'trial'), route)  1.74 us
    ppermute x1, starting transfers between devices, shards(): following = lax.ppermute(edge, ('tm', 'trial'), ring)  1.04 us
    ppermute x1, starting transfers between devices, shards(): received += [*both, lax.ppermute(handed, 'trial', [(0, 1), (1, 0)])]  0.37 us
  transfers between devices with their start and end apart: 5, of which 2 were waited for; matrix products, arithmetic and copies ran while one was open for 0% of the time, Pallas kernels for 3%

profile of v6, /device:TPU:1, one launch (start us, length us, event | category | flops | bytes accessed | tf_op | source)
XLA Modules:
  0.0 17.6 jit_solution(1762452783822254273)
XLA Ops:
  0.0 1.0 %shard_map.55 = (bf16[64,128]{1,0:T(8,128)(2,1)S(1)}, bf16[64,1024]{1,0:T(8,128)(2,1)S(1)}, s32[64,256]{1,0:T(8,128)S(1)}, bf16[64,256]{1,0:T(8,128)(2,1)S(1)}, ...) custom-call(bf16[64,1024]{1,0:T(8,128)(2,1)} %x_hbm.1, s32[64,256]{1,0:T(8,128)} %bitcast.6, bf16[64,256]{1,0:T(8,128)(2,1)} %bitcast.7, ...), custom_call_target="tpu_custom_call" | custom-call | tf_op jit(solution)/shard_map/pallas_call | solution.py:198
  1.0 1.5 %shard_map.56 = (bf16[512,640]{1,0:T(8,128)(2,1)S(1)}, s32[8,128]{1,0:T(8,128)S(1)}, bf16[32,896]{1,0:T(8,128)(2,1)S(1)}, bf16[64,896]{1,0:T(8,128)(2,1)S(1)}, bf16[32,896]{1,0:T(8,128)(2,1)S(1)}) custom-call(bf16[64,1024]{1,0:T(8,128)(2,1)S(1)} %get-tuple-element.19.x_ref, s32[64,256]{1,0:T(8,128)S(1)} %get-tuple-element.20.off_ref, ...), custom_call_target="tpu_custom_call" | custom-call | tf_op jit(solution)/shard_map/pallas_call | solution.py:198
  2.5 3.2 %collective-permute-start.1 = (bf16[64,896]{1,0:T(8,128)(2,1)S(1)}, bf16[64,896]{1,0:T(8,128)(2,1)S(1)}, u32[]{:S(2)}, u32[]{:S(2)}) collective-permute-start(bf16[64,896]{1,0:T(8,128)(2,1)S(1)} %get-tuple-element.30), channel_id=1, source_target_pairs={{0,4},{1,9},{4,0},{5,13},{8,12},{9,1},{12,8},{13,5},{2,6},{3,11},{... | collective-permute-start | bytes 344072 | tf_op jit(solution)/shard_map/ppermute | solution.py:280
  5.7 1.0 %collective-permute-start = (bf16[64,128]{1,0:T(8,128)(2,1)S(1)}, bf16[64,128]{1,0:T(8,128)(2,1)S(1)}, u32[]{:S(2)}, u32[]{:S(2)}) collective-permute-start(bf16[64,128]{1,0:T(8,128)(2,1)S(1)} %get-tuple-element.25), channel_id=1, source_target_pairs={{3,0},{2,1},{1,2},{0,3},{7,4},{6,5},{5,6},{4,7},{11,8},{10,9},{9,1... | collective-permute-start | bytes 49160 | tf_op jit(solution)/shard_map/ppermute | solution.py:256
  6.7 2.4 %collective-permute-done.next_ref = bf16[64,128]{1,0:T(8,128)(2,1)S(1)} collective-permute-done((bf16[64,128]{1,0:T(8,128)(2,1)S(1)}, bf16[64,128]{1,0:T(8,128)(2,1)S(1)}, u32[]{:S(2)}, u32[]{:S(2)}) %collective-permute-start) | collective-permute-done | bytes 16416 | tf_op jit(solution)/shard_map/ppermute | solution.py:256
  9.1 0.5 %shard_map.57 = (bf16[32,128]{1,0:T(8,128)(2,1)S(1)}, bf16[64,128]{1,0:T(8,128)(2,1)S(1)}, bf16[32,1024]{1,0:T(8,128)(2,1)S(1)}) custom-call(bf16[64,1024]{1,0:T(8,128)(2,1)S(1)} %get-tuple-element.19.x_ref, bf16[64,128]{1,0:T(8,128)(2,1)S(1)} %collective-permute-done.next_ref, bf16[512,640]{1,0:T(8,128)(2,1)S(1)} %get-tuple-element.26.rhs_ref, ...), custom_call_target="tpu_custom_call" | custom-call | tf_op jit(solution)/shard_map/pallas_call | solution.py:198
  9.6 1.8 %collective-permute-start.2 = (bf16[64,128]{1,0:T(8,128)(2,1)S(1)}, bf16[64,128]{1,0:T(8,128)(2,1)S(1)}, u32[]{:S(2)}, u32[]{:S(2)}) collective-permute-start(bf16[64,128]{1,0:T(8,128)(2,1)S(1)} %get-tuple-element.31), channel_id=1, source_target_pairs={{0,4},{1,9},{4,0},{5,13},{8,12},{9,1},{12,8},{13,5},{2,6},{3,11},{... | collective-permute-start | bytes 49160 | tf_op jit(solution)/shard_map/ppermute | solution.py:280
  11.4 1.7 %collective-permute-start.4 = (bf16[32,1024]{1,0:T(8,128)(2,1)S(1)}, bf16[32,1024]{1,0:T(8,128)(2,1)S(1)}, u32[]{:S(2)}, u32[]{:S(2)}) collective-permute-start(bf16[32,1024]{1,0:T(8,128)(2,1)S(1)} %get-tuple-element.32), channel_id=1, source_target_pairs={{0,13},{1,12},{4,9},{5,8},{8,5},{9,4},{12,1},{13,0},{2,15},{3,14},... | collective-permute-start | bytes 196616 | tf_op jit(solution)/shard_map/ppermute | solution.py:297
  13.2 0.0 collective-permute-done.2.tail_ref.refs_3_
  13.2 0.0 collective-permute-done.1.body_ref.refs_2_
  13.2 0.4 %collective-permute-start.3 = (bf16[32,1024]{1,0:T(8,128)(2,1)S(1)}, bf16[32,1024]{1,0:T(8,128)(2,1)S(1)}, u32[]{:S(2)}, u32[]{:S(2)}) collective-permute-start(bf16[32,1024]{1,0:T(8,128)(2,1)S(1)} %shard_map.58), channel_id=1, source_target_pairs={{0,1},{1,0},{2,3},{3,2},{4,5},{5,4},{6,7},{7,6},{8,9},{9,8},{10,11... | collective-permute-start | bytes 196616 | tf_op jit(solution)/shard_map/ppermute | solution.py:301
  13.6 3.3 %collective-permute-done.4.refs_5_ = bf16[32,1024]{1,0:T(8,128)(2,1)S(1)} collective-permute-done((bf16[32,1024]{1,0:T(8,128)(2,1)S(1)}, bf16[32,1024]{1,0:T(8,128)(2,1)S(1)}, u32[]{:S(2)}, u32[]{:S(2)}) %collective-permute-start.4) | collective-permute-done | bytes 65568 | tf_op jit(solution)/shard_map/ppermute | solution.py:297
  16.9 0.0 collective-permute-done.3.refs_4_
  16.9 0.7 %shard_map.59 = bf16[32,1024]{1,0:T(8,128)(2,1)} custom-call(bf16[32,896]{1,0:T(8,128)(2,1)S(1)} %get-tuple-element.24.refs_0_, bf16[32,128]{1,0:T(8,128)(2,1)S(1)} %get-tuple-element.29.refs_1_, bf16[64,896]{1,0:T(8,128)(2,1)S(1)} %collective-permute-done.1.body_ref.refs_2_, bf16[64,128]{1,0:T(8,128)(2,1)S(1)} %collective-permute-done.2.tail_ref.refs_3_, ...), custom_call_target="tpu_custom_call" | custom-call | tf_op jit(solution)/shard_map/pallas_call | solution.py:198
  (1 shorter events, 0.0 us)
Async XLA Ops:
  2.5 10.7 %collective-permute-start.1 = (bf16[64,896]{1,0:T(8,128)(2,1)S(1)}, bf16[64,896]{1,0:T(8,128)(2,1)S(1)}, u32[]{:S(2)}, u32[]{:S(2)}) collective-permute-start(bf16[64,896]{1,0:T(8,128)(2,1)S(1)} %get-tuple-element.30), channel_id=1, source_target_pairs={{0,4},{1,9},{4,0},{5,13},{8,12},{9,1},{12,8},{13,5},{2,6},{3,11},{... | collective-permute-start | bytes 344072 | tf_op jit(solution)/shard_map/ppermute | solution.py:280
  5.7 3.4 %collective-permute-start = (bf16[64,128]{1,0:T(8,128)(2,1)S(1)}, bf16[64,128]{1,0:T(8,128)(2,1)S(1)}, u32[]{:S(2)}, u32[]{:S(2)}) collective-permute-start(bf16[64,128]{1,0:T(8,128)(2,1)S(1)} %get-tuple-element.25), channel_id=1, source_target_pairs={{3,0},{2,1},{1,2},{0,3},{7,4},{6,5},{5,6},{4,7},{11,8},{10,9},{9,1... | collective-permute-start | bytes 49160 | tf_op jit(solution)/shard_map/ppermute | solution.py:256
  9.6 3.6 %collective-permute-start.2 = (bf16[64,128]{1,0:T(8,128)(2,1)S(1)}, bf16[64,128]{1,0:T(8,128)(2,1)S(1)}, u32[]{:S(2)}, u32[]{:S(2)}) collective-permute-start(bf16[64,128]{1,0:T(8,128)(2,1)S(1)} %get-tuple-element.31), channel_id=1, source_target_pairs={{0,4},{1,9},{4,0},{5,13},{8,12},{9,1},{12,8},{13,5},{2,6},{3,11},{... | collective-permute-start | bytes 49160 | tf_op jit(solution)/shard_map/ppermute | solution.py:280
  11.4 5.5 %collective-permute-start.4 = (bf16[32,1024]{1,0:T(8,128)(2,1)S(1)}, bf16[32,1024]{1,0:T(8,128)(2,1)S(1)}, u32[]{:S(2)}, u32[]{:S(2)}) collective-permute-start(bf16[32,1024]{1,0:T(8,128)(2,1)S(1)} %get-tuple-element.32), channel_id=1, source_target_pairs={{0,13},{1,12},{4,9},{5,8},{8,5},{9,4},{12,1},{13,0},{2,15},{3,14},... | collective-permute-start | bytes 196616 | tf_op jit(solution)/shard_map/ppermute | solution.py:297
  13.2 3.7 %collective-permute-start.3 = (bf16[32,1024]{1,0:T(8,128)(2,1)S(1)}, bf16[32,1024]{1,0:T(8,128)(2,1)S(1)}, u32[]{:S(2)}, u32[]{:S(2)}) collective-permute-start(bf16[32,1024]{1,0:T(8,128)(2,1)S(1)} %shard_map.58), channel_id=1, source_target_pairs={{0,1},{1,0},{2,3},{3,2},{4,5},{5,4},{6,7},{7,6},{8,9},{9,8},{10,11... | collective-permute-start | bytes 196616 | tf_op jit(solution)/shard_map/ppermute | solution.py:301

commit v7 on v6

--- a/solution.py
+++ b/solution.py
@@ -117,34 +117,28 @@
             out_ref[:, index * LANES : (index + 1) * LANES] = block[rows]
 
 
-def load_kernel(x_hbm, off_hbm, wt_hbm, map_hbm, del_hbm, edge_ref, x_ref, off_ref, wt_ref, map_ref, del_ref, sems):
-    moves = [
-        pltpu.make_async_copy(source, target, sems.at[index])
-        for index, (source, target) in enumerate(
-            (
-                (x_hbm, x_ref),
-                (off_hbm, off_ref),
-                (wt_hbm, wt_ref),
-                (map_hbm, map_ref),
-                (del_hbm, del_ref),
-            )
-        )
-    ]
+def load_kernel(
+    freq_count, x_hbm, off_hbm, wt_hbm, map_hbm, del_hbm, edge_ref, x_ref, off_ref, wt_ref, mine_ref, map_ref, del_ref, sems
+):
+    targets = ((map_hbm, map_ref), (del_hbm, del_ref), (x_hbm, x_ref), (off_hbm, off_ref), (wt_hbm, wt_ref))
+    moves = [pltpu.make_async_copy(source, target, sems.at[k]) for k, (source, target) in enumerate(targets)]
     for move in moves:
         move.start()
-    moves[0].wait()
+    for move in moves[:2]:
+        move.wait()
+    mine_ref[...] = own_columns(freq_count, map_ref, del_ref)
+    moves[2].wait()
     edge_ref[...] = x_ref[:, : edge_ref.shape[1]]
-    for move in moves[1:]:
+    for move in moves[3:]:
         move.wait()
 
 
 def main_kernel(
-    freq_count, x_ref, off_ref, wt_ref, map_ref, del_ref, rhs_ref, delay_ref, *rest
+    freq_count, x_ref, off_ref, wt_ref, mine_ref, rhs_ref, *rest
 ):
     outs, (time_ref, lhs_ref, plane_ref, leaf_ref) = rest[:-4], rest[-4:]
-    mine = own_columns(freq_count, map_ref, del_ref)
+    mine = mine_ref[...]
     build_taps(off_ref, wt_ref, mine, rhs_ref)
-    delay_ref[...] = mine
     columns = outs[0].shape[1]
     span = (freq_count.bit_length() - 1) * SHIFT
     blocks = convolve(x_ref[...], span, columns, mine[1:2, :], rhs_ref, time_ref, lhs_ref, plane_ref, leaf_ref)
@@ -171,24 +165,29 @@
     out_ref[:, body:] = tail_ref[piece:, :]
 
 
-def final_kernel(freq_count, *refs):
-    out_ref = refs[-1]
+def final_kernel(*refs):
+    own_refs, far_ref, out_ref = refs[:2], refs[-2], refs[-1]
+    pair_refs = [refs[k : k + 3] for k in range(2, len(refs) - 2, 3)]
     piece, seg = out_ref.shape
     body = refs[0].shape[1]
-    first_core = lax.axis_index("trial") == 0
-    for part, columns in ((0, slice(0, body)), (1, slice(body, seg))):
-        planes = [refs[part][...].astype(jnp.float32)]
-        for pair in range(len(shared_pairs(freq_count))):
-            here = refs[2 + 3 * pair + part][:piece, :].astype(jnp.float32)
-            there = refs[2 + 3 * pair + 2][:, columns].astype(jnp.float32)
-            planes += [jnp.where(first_core, here, there), jnp.where(first_core, there, here)]
-        planes.append(refs[-2][:, columns].astype(jnp.float32))
-        while len(planes) > 1:
-            planes = [
-                (lower + upper).astype(jnp.bfloat16).astype(jnp.float32)
-                for lower, upper in zip(planes[::2], planes[1::2])
-            ]
-        out_ref[:, columns] = planes[0].astype(jnp.bfloat16)
+
+    def add_up(first_core):
+        for part, columns in ((0, slice(0, body)), (1, slice(body, seg))):
+            planes = [own_refs[part][...]]
+            for pair in pair_refs:
+                here, there = pair[part][:piece, :], pair[2][:, columns]
+                planes += [here, there] if first_core else [there, here]
+            planes.append(far_ref[:, columns])
+            while len(planes) > 1:
+                planes = [
+                    (lower.astype(jnp.float32) + upper.astype(jnp.float32)).astype(jnp.bfloat16)
+                    for lower, upper in zip(planes[::2], planes[1::2])
+                ]
+            out_ref[:, columns] = planes[0]
+
+    core = lax.axis_index("trial")
+    pl.when(core == 0)(lambda: add_up(True))
+    pl.when(core != 0)(lambda: add_up(False))
 
 
 def call(kernel, outs, *args, scratch=(), limit=16 << 20, space=None):
@@ -230,22 +229,25 @@
             pltpu.VMEM((leaf_rows, rows), jnp.float32),
         )
 
-    edge, samples, lags, weights, chosen, lateness = call(
-        load_kernel,
+    edge, samples, lags, weights, columns = call(
+        functools.partial(load_kernel, freq_count),
         [
             plane_of(band, tail),
             plane_of(band, seg),
             jax.ShapeDtypeStruct((band, trials), jnp.int32),
             plane_of(band, trials),
-            jax.ShapeDtypeStruct((1, trials), jnp.int32),
-            jax.ShapeDtypeStruct(delays.shape, jnp.int32),
+            jax.ShapeDtypeStruct((8, rows), jnp.int32),
         ],
         spectra,
         jnp.swapaxes(tap_offsets[0], 0, 1),
         jnp.swapaxes(tap_weights[0], 0, 1),
         trial_map,
         delays,
-        scratch=(pltpu.SemaphoreType.DMA((5,)),),
+        scratch=(
+            pltpu.VMEM((1, trials), jnp.int32),
+            pltpu.VMEM(delays.shape, jnp.int32),
+            pltpu.SemaphoreType.DMA((5,)),
+        ),
         space=pltpu.HBM,
     )
     ring = [
@@ -257,18 +259,16 @@
     piece = rows // freq_count
     pairs = shared_pairs(freq_count)
     heights = [piece, *[2 * piece] * len(pairs), piece]
-    taps, columns, *bodies = call(
+    taps, *bodies = call(
         functools.partial(main_kernel, freq_count),
         [
             plane_of(FINE * band, PLANES * rows),
-            jax.ShapeDtypeStruct((8, rows), jnp.int32),
             *[plane_of(height, body) for height in heights],
         ],
         samples,
         lags,
         weights,
-        chosen,
-        lateness,
+        columns,
         scratch=scratch(body),
     )
     devices = [(f, c) for f in range(freq_count) for c in range(core_count)]
@@ -299,7 +299,7 @@
     for both in zip(bodies, tails):
         handed = call(second_half_kernel, plane_of(piece, seg), *both)
         received += [*both, lax.ppermute(handed, "trial", [(0, 1), (1, 0)])]
-    return call(functools.partial(final_kernel, freq_count), plane_of(piece, seg), own, own_tail, *received, far)
+    return call(final_kernel, plane_of(piece, seg), own, own_tail, *received, far)
 
 
 def solution(mesh):

time: 17.8 us -> 17.7 us (level)
  no operation moved by 1% of the time
where the time goes in v7:
time: 17.7 us; the launch traced here: 17.5 us
  starting transfers between devices  8.12 us (46%)
  waiting for transfers between devices  5.77 us (33%)
  Pallas kernels  3.61 us (20%)
    ppermute x2, starting transfers between devices, traded(): arrived.append(lax.ppermute(block, ('freq', 'trial'), route))  4.97 us
    pallas_call x5, Pallas kernels, call(): pl.pallas_call(kernel, out_shape=outs, **specs, scratch_shapes=list(scrat...  3.61 us
    ppermute x1, waiting for transfers between devices, shards(): far = lax.ppermute(far, ('freq', 'trial'), route)  3.32 us
    ppermute x1, waiting for transfers between devices, shards(): following = lax.ppermute(edge, ('tm', 'trial'), ring)  2.4 us
    ppermute x1, starting transfers between devices, shards(): far = lax.ppermute(far, ('freq', 'trial'), route)  1.74 us
    ppermute x1, starting transfers between devices, shards(): following = lax.ppermute(edge, ('tm', 'trial'), ring)  1.04 us
    ppermute x1, starting transfers between devices, shards(): received += [*both, lax.ppermute(handed, 'trial', [(0, 1), (1, 0)])]  0.37 us
  transfers between devices with their start and end apart: 5, of which 2 were waited for; matrix products, arithmetic and copies ran while one was open for 0% of the time, Pallas kernels for 3%

profile of v7, /device:TPU:1, one launch (start us, length us, event | category | flops | bytes accessed | tf_op | source)
XLA Modules:
  0.0 17.5 jit_solution(16714285952188984533)
XLA Ops:
  0.0 1.0 %shard_map.55 = (bf16[64,128]{1,0:T(8,128)(2,1)S(1)}, bf16[64,1024]{1,0:T(8,128)(2,1)S(1)}, s32[64,256]{1,0:T(8,128)S(1)}, bf16[64,256]{1,0:T(8,128)(2,1)S(1)}, s32[8,128]{1,0:T(8,128)S(1)}) custom-call(bf16[64,1024]{1,0:T(8,128)(2,1)} %x_hbm.1, s32[64,256]{1,0:T(8,128)} %bitcast.6, bf16[64,256]{1,0:T(8,128)(2,1)} %bitcast.7, s32[1,256]{1,0:T(1,128)} %map_hbm.1, ...), custom_call_target="tpu_custom_call" | custom-call | tf_op jit(solution)/shard_map/pallas_call | solution.py:197
  1.0 1.4 %shard_map.56 = (bf16[512,640]{1,0:T(8,128)(2,1)S(1)}, bf16[32,896]{1,0:T(8,128)(2,1)S(1)}, bf16[64,896]{1,0:T(8,128)(2,1)S(1)}, bf16[32,896]{1,0:T(8,128)(2,1)S(1)}) custom-call(bf16[64,1024]{1,0:T(8,128)(2,1)S(1)} %get-tuple-element.17.x_ref, s32[64,256]{1,0:T(8,128)S(1)} %get-tuple-element.18.off_ref, bf16[64,256]{1,0:T(8,128)(2,1)S(1)} %get-tuple-element.19.wt_ref, ...), custom_call_target="tpu_custom_call" | custom-call | tf_op jit(solution)/shard_map/pallas_call | solution.py:197
  2.4 3.2 %collective-permute-start.1 = (bf16[64,896]{1,0:T(8,128)(2,1)S(1)}, bf16[64,896]{1,0:T(8,128)(2,1)S(1)}, u32[]{:S(2)}, u32[]{:S(2)}) collective-permute-start(bf16[64,896]{1,0:T(8,128)(2,1)S(1)} %get-tuple-element.26), channel_id=1, source_target_pairs={{0,4},{1,9},{4,0},{5,13},{8,12},{9,1},{12,8},{13,5},{2,6},{3,11},{... | collective-permute-start | bytes 344072 | tf_op jit(solution)/shard_map/ppermute | solution.py:280
  5.6 1.0 %collective-permute-start = (bf16[64,128]{1,0:T(8,128)(2,1)S(1)}, bf16[64,128]{1,0:T(8,128)(2,1)S(1)}, u32[]{:S(2)}, u32[]{:S(2)}) collective-permute-start(bf16[64,128]{1,0:T(8,128)(2,1)S(1)} %get-tuple-element.22), channel_id=1, source_target_pairs={{3,0},{2,1},{1,2},{0,3},{7,4},{6,5},{5,6},{4,7},{11,8},{10,9},{9,1... | collective-permute-start | bytes 49160 | tf_op jit(solution)/shard_map/ppermute | solution.py:258
  6.7 2.4 %collective-permute-done.next_ref = bf16[64,128]{1,0:T(8,128)(2,1)S(1)} collective-permute-done((bf16[64,128]{1,0:T(8,128)(2,1)S(1)}, bf16[64,128]{1,0:T(8,128)(2,1)S(1)}, u32[]{:S(2)}, u32[]{:S(2)}) %collective-permute-start) | collective-permute-done | bytes 16416 | tf_op jit(solution)/shard_map/ppermute | solution.py:258
  9.1 0.5 %shard_map.57 = (bf16[32,128]{1,0:T(8,128)(2,1)S(1)}, bf16[64,128]{1,0:T(8,128)(2,1)S(1)}, bf16[32,1024]{1,0:T(8,128)(2,1)S(1)}) custom-call(bf16[64,1024]{1,0:T(8,128)(2,1)S(1)} %get-tuple-element.17.x_ref, bf16[64,128]{1,0:T(8,128)(2,1)S(1)} %collective-permute-done.next_ref, bf16[512,640]{1,0:T(8,128)(2,1)S(1)} %get-tuple-element.23.rhs_ref, ...), custom_call_target="tpu_custom_call" | custom-call | tf_op jit(solution)/shard_map/pallas_call | solution.py:197
  9.6 1.8 %collective-permute-start.2 = (bf16[64,128]{1,0:T(8,128)(2,1)S(1)}, bf16[64,128]{1,0:T(8,128)(2,1)S(1)}, u32[]{:S(2)}, u32[]{:S(2)}) collective-permute-start(bf16[64,128]{1,0:T(8,128)(2,1)S(1)} %get-tuple-element.27), channel_id=1, source_target_pairs={{0,4},{1,9},{4,0},{5,13},{8,12},{9,1},{12,8},{13,5},{2,6},{3,11},{... | collective-permute-start | bytes 49160 | tf_op jit(solution)/shard_map/ppermute | solution.py:280
  11.4 1.7 %collective-permute-start.4 = (bf16[32,1024]{1,0:T(8,128)(2,1)S(1)}, bf16[32,1024]{1,0:T(8,128)(2,1)S(1)}, u32[]{:S(2)}, u32[]{:S(2)}) collective-permute-start(bf16[32,1024]{1,0:T(8,128)(2,1)S(1)} %get-tuple-element.28), channel_id=1, source_target_pairs={{0,13},{1,12},{4,9},{5,8},{8,5},{9,4},{12,1},{13,0},{2,15},{3,14},... | collective-permute-start | bytes 196616 | tf_op jit(solution)/shard_map/ppermute | solution.py:297
  13.1 0.0 collective-permute-done.2.tail_ref.refs_3_
  13.1 0.0 collective-permute-done.1.body_ref.refs_2_
  13.1 0.4 %collective-permute-start.3 = (bf16[32,1024]{1,0:T(8,128)(2,1)S(1)}, bf16[32,1024]{1,0:T(8,128)(2,1)S(1)}, u32[]{:S(2)}, u32[]{:S(2)}) collective-permute-start(bf16[32,1024]{1,0:T(8,128)(2,1)S(1)} %shard_map.58), channel_id=1, source_target_pairs={{0,1},{1,0},{2,3},{3,2},{4,5},{5,4},{6,7},{7,6},{8,9},{9,8},{10,11... | collective-permute-start | bytes 196616 | tf_op jit(solution)/shard_map/ppermute | solution.py:301
  13.5 3.3 %collective-permute-done.4.refs_5_ = bf16[32,1024]{1,0:T(8,128)(2,1)S(1)} collective-permute-done((bf16[32,1024]{1,0:T(8,128)(2,1)S(1)}, bf16[32,1024]{1,0:T(8,128)(2,1)S(1)}, u32[]{:S(2)}, u32[]{:S(2)}) %collective-permute-start.4) | collective-permute-done | bytes 65568 | tf_op jit(solution)/shard_map/ppermute | solution.py:297
  16.8 0.0 collective-permute-done.3.refs_4_
  16.8 0.7 %shard_map.59 = bf16[32,1024]{1,0:T(8,128)(2,1)} custom-call(bf16[32,896]{1,0:T(8,128)(2,1)S(1)} %get-tuple-element.21.refs_0_, bf16[32,128]{1,0:T(8,128)(2,1)S(1)} %get-tuple-element.25.refs_1_, bf16[64,896]{1,0:T(8,128)(2,1)S(1)} %collective-permute-done.1.body_ref.refs_2_, bf16[64,128]{1,0:T(8,128)(2,1)S(1)} %collective-permute-done.2.tail_ref.refs_3_, ...), custom_call_target="tpu_custom_call" | custom-call | tf_op jit(solution)/shard_map/pallas_call | solution.py:197
  (1 shorter events, 0.0 us)
Async XLA Ops:
  2.4 10.7 %collective-permute-start.1 = (bf16[64,896]{1,0:T(8,128)(2,1)S(1)}, bf16[64,896]{1,0:T(8,128)(2,1)S(1)}, u32[]{:S(2)}, u32[]{:S(2)}) collective-permute-start(bf16[64,896]{1,0:T(8,128)(2,1)S(1)} %get-tuple-element.26), channel_id=1, source_target_pairs={{0,4},{1,9},{4,0},{5,13},{8,12},{9,1},{12,8},{13,5},{2,6},{3,11},{... | collective-permute-start | bytes 344072 | tf_op jit(solution)/shard_map/ppermute | solution.py:280
  5.6 3.4 %collective-permute-start = (bf16[64,128]{1,0:T(8,128)(2,1)S(1)}, bf16[64,128]{1,0:T(8,128)(2,1)S(1)}, u32[]{:S(2)}, u32[]{:S(2)}) collective-permute-start(bf16[64,128]{1,0:T(8,128)(2,1)S(1)} %get-tuple-element.22), channel_id=1, source_target_pairs={{3,0},{2,1},{1,2},{0,3},{7,4},{6,5},{5,6},{4,7},{11,8},{10,9},{9,1... | collective-permute-start | bytes 49160 | tf_op jit(solution)/shard_map/ppermute | solution.py:258
  9.6 3.6 %collective-permute-start.2 = (bf16[64,128]{1,0:T(8,128)(2,1)S(1)}, bf16[64,128]{1,0:T(8,128)(2,1)S(1)}, u32[]{:S(2)}, u32[]{:S(2)}) collective-permute-start(bf16[64,128]{1,0:T(8,128)(2,1)S(1)} %get-tuple-element.27), channel_id=1, source_target_pairs={{0,4},{1,9},{4,0},{5,13},{8,12},{9,1},{12,8},{13,5},{2,6},{3,11},{... | collective-permute-start | bytes 49160 | tf_op jit(solution)/shard_map/ppermute | solution.py:280
  11.4 5.5 %collective-permute-start.4 = (bf16[32,1024]{1,0:T(8,128)(2,1)S(1)}, bf16[32,1024]{1,0:T(8,128)(2,1)S(1)}, u32[]{:S(2)}, u32[]{:S(2)}) collective-permute-start(bf16[32,1024]{1,0:T(8,128)(2,1)S(1)} %get-tuple-element.28), channel_id=1, source_target_pairs={{0,13},{1,12},{4,9},{5,8},{8,5},{9,4},{12,1},{13,0},{2,15},{3,14},... | collective-permute-start | bytes 196616 | tf_op jit(solution)/shard_map/ppermute | solution.py:297
  13.1 3.7 %collective-permute-start.3 = (bf16[32,1024]{1,0:T(8,128)(2,1)S(1)}, bf16[32,1024]{1,0:T(8,128)(2,1)S(1)}, u32[]{:S(2)}, u32[]{:S(2)}) collective-permute-start(bf16[32,1024]{1,0:T(8,128)(2,1)S(1)} %shard_map.58), channel_id=1, source_target_pairs={{0,1},{1,0},{2,3},{3,2},{4,5},{5,4},{6,7},{7,6},{8,9},{9,8},{10,11... | collective-permute-start | bytes 196616 | tf_op jit(solution)/shard_map/ppermute | solution.py:301

commit v8 on v7

--- a/solution.py
+++ b/solution.py
@@ -38,9 +38,11 @@
     core_index = lax.axis_index("trial")
     total = jnp.zeros((1, trials), jnp.int32)
     for level in range(levels):
-        node = freq_count - (freq_count >> level) + lax.shift_right_logical(freq_index, level + 1)
-        bit = lax.shift_right_logical(freq_index, level) & 1
-        total = total + del_ref[pl.ds(node, 1), :] * bit
+        first_node = freq_count - (freq_count >> level)
+        pair = lax.shift_right_logical(freq_index, level + 1)
+        upper = lax.shift_right_logical(freq_index, level) & 1
+        for k in range(freq_count >> level + 1):
+            total = total + del_ref[first_node + k : first_node + k + 1, :] * jnp.where(pair == k, upper, 0)
     first = lax.broadcasted_iota(jnp.int32, (8, trials), 0) == 0
     both = jnp.where(
         first, jnp.broadcast_to(map_ref[...], (8, trials)), jnp.broadcast_to(total, (8, trials))
@@ -61,13 +63,14 @@
     picker = picker.astype(jnp.float32).astype(jnp.bfloat16)
     tables = jnp.concatenate([wt_ref[...], off_ref[...].astype(jnp.float32).astype(jnp.bfloat16)], axis=0)
     picked = jnp.dot(tables, picker, preferred_element_type=jnp.float32)
-    weights = picked[:band]
-    lags = picked[band:].astype(jnp.int32) + (mine[1:2, :] & (FINE - 1))
+    weights = picked[:band].astype(jnp.bfloat16)
+    lags = (picked[band:] + (mine[1:2, :] & (FINE - 1)).astype(jnp.float32)).astype(jnp.bfloat16)
+    zero = jnp.zeros_like(weights)
     for fine in range(FINE):
         for plane in range(PLANES):
             rhs_ref[fine * band : (fine + 1) * band, plane * rows : (plane + 1) * rows] = jnp.where(
-                lags == plane * FINE + fine, weights, 0.0
-            ).astype(jnp.bfloat16)
+                lags == plane * FINE + fine, weights, zero
+            )
 
 
 def convolve(window, span, columns, delay_row, rhs_ref, time_ref, lhs_ref, plane_ref, leaf_ref):
@@ -76,7 +79,7 @@
     leaf_rows = columns + span
     lhs_rows = leaf_rows + FINE * (PLANES - 1)
     time_rows = lhs_rows + FINE
-    turned = jnp.transpose(jnp.concatenate([window] * (LANES // band), axis=0).astype(jnp.float32))
+    turned = jnp.transpose(jnp.concatenate([window] * (LANES // band), axis=0)).astype(jnp.float32)
     time_ref[:time_rows, :] = turned[:time_rows, :]
     low_lanes = lax.broadcasted_iota(jnp.int32, (lhs_rows, LANES), 1) < band
     for pair in range(FINE // 2):
@@ -104,7 +107,7 @@
             if moved.shape[0] < length:
                 moved = jnp.concatenate([moved, jnp.zeros((length - moved.shape[0], rows), jnp.float32)], axis=0)
             part = jnp.where(take, moved, part[:length])
-        blocks.append(jnp.transpose(part[:LANES]).astype(jnp.bfloat16))
+        blocks.append(jnp.transpose(part[:LANES].astype(jnp.bfloat16)))
     return blocks
 
 

time: 17.7 us -> 17.6 us (level)
  no operation moved by 1% of the time
where the time goes in v8:
time: 17.6 us; the launch traced here: 17.4 us
  starting transfers between devices  8.12 us (46%)
  waiting for transfers between devices  5.77 us (33%)
  Pallas kernels  3.49 us (20%)
    ppermute x2, starting transfers between devices, traded(): arrived.append(lax.ppermute(block, ('freq', 'trial'), route))  4.97 us
    pallas_call x5, Pallas kernels, call(): pl.pallas_call(kernel, out_shape=outs, **specs, scratch_shapes=list(scrat...  3.49 us
    ppermute x1, waiting for transfers between devices, shards(): far = lax.ppermute(far, ('freq', 'trial'), route)  3.33 us
    ppermute x1, waiting for transfers between devices, shards(): following = lax.ppermute(edge, ('tm', 'trial'), ring)  2.4 us
    ppermute x1, starting transfers between devices, shards(): far = lax.ppermute(far, ('freq', 'trial'), route)  1.74 us
    ppermute x1, starting transfers between devices, shards(): following = lax.ppermute(edge, ('tm', 'trial'), ring)  1.04 us
    ppermute x1, starting transfers between devices, shards(): received += [*both, lax.ppermute(handed, 'trial', [(0, 1), (1, 0)])]  0.37 us
  transfers between devices with their start and end apart: 5, of which 2 were waited for; matrix products, arithmetic and copies ran while one was open for 0% of the time, Pallas kernels for 3%

profile of v8, /device:TPU:1, one launch (start us, length us, event | category | flops | bytes accessed | tf_op | source)
XLA Modules:
  0.0 17.4 jit_solution(16382225622893605602)
XLA Ops:
  0.0 1.0 %shard_map.55 = (bf16[64,128]{1,0:T(8,128)(2,1)S(1)}, bf16[64,1024]{1,0:T(8,128)(2,1)S(1)}, s32[64,256]{1,0:T(8,128)S(1)}, bf16[64,256]{1,0:T(8,128)(2,1)S(1)}, s32[8,128]{1,0:T(8,128)S(1)}) custom-call(bf16[64,1024]{1,0:T(8,128)(2,1)} %x_hbm.1, s32[64,256]{1,0:T(8,128)} %bitcast.6, bf16[64,256]{1,0:T(8,128)(2,1)} %bitcast.7, s32[1,256]{1,0:T(1,128)} %map_hbm.1, ...), custom_call_target="tpu_custom_call" | custom-call | tf_op jit(solution)/shard_map/pallas_call | solution.py:200
  1.0 1.3 %shard_map.56 = (bf16[512,640]{1,0:T(8,128)(2,1)S(1)}, bf16[32,896]{1,0:T(8,128)(2,1)S(1)}, bf16[64,896]{1,0:T(8,128)(2,1)S(1)}, bf16[32,896]{1,0:T(8,128)(2,1)S(1)}) custom-call(bf16[64,1024]{1,0:T(8,128)(2,1)S(1)} %get-tuple-element.17.x_ref, s32[64,256]{1,0:T(8,128)S(1)} %get-tuple-element.18.off_ref, bf16[64,256]{1,0:T(8,128)(2,1)S(1)} %get-tuple-element.19.wt_ref, ...), custom_call_target="tpu_custom_call" | custom-call | tf_op jit(solution)/shard_map/pallas_call | solution.py:200
  2.3 3.2 %collective-permute-start.1 = (bf16[64,896]{1,0:T(8,128)(2,1)S(1)}, bf16[64,896]{1,0:T(8,128)(2,1)S(1)}, u32[]{:S(2)}, u32[]{:S(2)}) collective-permute-start(bf16[64,896]{1,0:T(8,128)(2,1)S(1)} %get-tuple-element.26), channel_id=1, source_target_pairs={{0,4},{1,9},{4,0},{5,13},{8,12},{9,1},{12,8},{13,5},{2,6},{3,11},{... | collective-permute-start | bytes 344072 | tf_op jit(solution)/shard_map/ppermute | solution.py:283
  5.5 1.0 %collective-permute-start = (bf16[64,128]{1,0:T(8,128)(2,1)S(1)}, bf16[64,128]{1,0:T(8,128)(2,1)S(1)}, u32[]{:S(2)}, u32[]{:S(2)}) collective-permute-start(bf16[64,128]{1,0:T(8,128)(2,1)S(1)} %get-tuple-element.22), channel_id=1, source_target_pairs={{3,0},{2,1},{1,2},{0,3},{7,4},{6,5},{5,6},{4,7},{11,8},{10,9},{9,1... | collective-permute-start | bytes 49160 | tf_op jit(solution)/shard_map/ppermute | solution.py:261
  6.6 2.4 %collective-permute-done.next_ref = bf16[64,128]{1,0:T(8,128)(2,1)S(1)} collective-permute-done((bf16[64,128]{1,0:T(8,128)(2,1)S(1)}, bf16[64,128]{1,0:T(8,128)(2,1)S(1)}, u32[]{:S(2)}, u32[]{:S(2)}) %collective-permute-start) | collective-permute-done | bytes 16416 | tf_op jit(solution)/shard_map/ppermute | solution.py:261
  9.0 0.5 %shard_map.57 = (bf16[32,128]{1,0:T(8,128)(2,1)S(1)}, bf16[64,128]{1,0:T(8,128)(2,1)S(1)}, bf16[32,1024]{1,0:T(8,128)(2,1)S(1)}) custom-call(bf16[64,1024]{1,0:T(8,128)(2,1)S(1)} %get-tuple-element.17.x_ref, bf16[64,128]{1,0:T(8,128)(2,1)S(1)} %collective-permute-done.next_ref, bf16[512,640]{1,0:T(8,128)(2,1)S(1)} %get-tuple-element.23.rhs_ref, ...), custom_call_target="tpu_custom_call" | custom-call | tf_op jit(solution)/shard_map/pallas_call | solution.py:200
  9.5 1.8 %collective-permute-start.2 = (bf16[64,128]{1,0:T(8,128)(2,1)S(1)}, bf16[64,128]{1,0:T(8,128)(2,1)S(1)}, u32[]{:S(2)}, u32[]{:S(2)}) collective-permute-start(bf16[64,128]{1,0:T(8,128)(2,1)S(1)} %get-tuple-element.27), channel_id=1, source_target_pairs={{0,4},{1,9},{4,0},{5,13},{8,12},{9,1},{12,8},{13,5},{2,6},{3,11},{... | collective-permute-start | bytes 49160 | tf_op jit(solution)/shard_map/ppermute | solution.py:283
  11.2 1.7 %collective-permute-start.4 = (bf16[32,1024]{1,0:T(8,128)(2,1)S(1)}, bf16[32,1024]{1,0:T(8,128)(2,1)S(1)}, u32[]{:S(2)}, u32[]{:S(2)}) collective-permute-start(bf16[32,1024]{1,0:T(8,128)(2,1)S(1)} %get-tuple-element.28), channel_id=1, source_target_pairs={{0,13},{1,12},{4,9},{5,8},{8,5},{9,4},{12,1},{13,0},{2,15},{3,14},... | collective-permute-start | bytes 196616 | tf_op jit(solution)/shard_map/ppermute | solution.py:300
  13.0 0.0 collective-permute-done.2.tail_ref.refs_3_
  13.0 0.0 collective-permute-done.1.body_ref.refs_2_
  13.0 0.4 %collective-permute-start.3 = (bf16[32,1024]{1,0:T(8,128)(2,1)S(1)}, bf16[32,1024]{1,0:T(8,128)(2,1)S(1)}, u32[]{:S(2)}, u32[]{:S(2)}) collective-permute-start(bf16[32,1024]{1,0:T(8,128)(2,1)S(1)} %shard_map.58), channel_id=1, source_target_pairs={{0,1},{1,0},{2,3},{3,2},{4,5},{5,4},{6,7},{7,6},{8,9},{9,8},{10,11... | collective-permute-start | bytes 196616 | tf_op jit(solution)/shard_map/ppermute | solution.py:304
  13.4 3.3 %collective-permute-done.4.refs_5_ = bf16[32,1024]{1,0:T(8,128)(2,1)S(1)} collective-permute-done((bf16[32,1024]{1,0:T(8,128)(2,1)S(1)}, bf16[32,1024]{1,0:T(8,128)(2,1)S(1)}, u32[]{:S(2)}, u32[]{:S(2)}) %collective-permute-start.4) | collective-permute-done | bytes 65568 | tf_op jit(solution)/shard_map/ppermute | solution.py:300
  16.7 0.0 collective-permute-done.3.refs_4_
  16.7 0.7 %shard_map.59 = bf16[32,1024]{1,0:T(8,128)(2,1)} custom-call(bf16[32,896]{1,0:T(8,128)(2,1)S(1)} %get-tuple-element.21.refs_0_, bf16[32,128]{1,0:T(8,128)(2,1)S(1)} %get-tuple-element.25.refs_1_, bf16[64,896]{1,0:T(8,128)(2,1)S(1)} %collective-permute-done.1.body_ref.refs_2_, bf16[64,128]{1,0:T(8,128)(2,1)S(1)} %collective-permute-done.2.tail_ref.refs_3_, ...), custom_call_target="tpu_custom_call" | custom-call | tf_op jit(solution)/shard_map/pallas_call | solution.py:200
  (1 shorter events, 0.0 us)
Async XLA Ops:
  2.3 10.7 %collective-permute-start.1 = (bf16[64,896]{1,0:T(8,128)(2,1)S(1)}, bf16[64,896]{1,0:T(8,128)(2,1)S(1)}, u32[]{:S(2)}, u32[]{:S(2)}) collective-permute-start(bf16[64,896]{1,0:T(8,128)(2,1)S(1)} %get-tuple-element.26), channel_id=1, source_target_pairs={{0,4},{1,9},{4,0},{5,13},{8,12},{9,1},{12,8},{13,5},{2,6},{3,11},{... | collective-permute-start | bytes 344072 | tf_op jit(solution)/shard_map/ppermute | solution.py:283
  5.5 3.4 %collective-permute-start = (bf16[64,128]{1,0:T(8,128)(2,1)S(1)}, bf16[64,128]{1,0:T(8,128)(2,1)S(1)}, u32[]{:S(2)}, u32[]{:S(2)}) collective-permute-start(bf16[64,128]{1,0:T(8,128)(2,1)S(1)} %get-tuple-element.22), channel_id=1, source_target_pairs={{3,0},{2,1},{1,2},{0,3},{7,4},{6,5},{5,6},{4,7},{11,8},{10,9},{9,1... | collective-permute-start | bytes 49160 | tf_op jit(solution)/shard_map/ppermute | solution.py:261
  9.5 3.6 %collective-permute-start.2 = (bf16[64,128]{1,0:T(8,128)(2,1)S(1)}, bf16[64,128]{1,0:T(8,128)(2,1)S(1)}, u32[]{:S(2)}, u32[]{:S(2)}) collective-permute-start(bf16[64,128]{1,0:T(8,128)(2,1)S(1)} %get-tuple-element.27), channel_id=1, source_target_pairs={{0,4},{1,9},{4,0},{5,13},{8,12},{9,1},{12,8},{13,5},{2,6},{3,11},{... | collective-permute-start | bytes 49160 | tf_op jit(solution)/shard_map/ppermute | solution.py:283
  11.2 5.5 %collective-permute-start.4 = (bf16[32,1024]{1,0:T(8,128)(2,1)S(1)}, bf16[32,1024]{1,0:T(8,128)(2,1)S(1)}, u32[]{:S(2)}, u32[]{:S(2)}) collective-permute-start(bf16[32,1024]{1,0:T(8,128)(2,1)S(1)} %get-tuple-element.28), channel_id=1, source_target_pairs={{0,13},{1,12},{4,9},{5,8},{8,5},{9,4},{12,1},{13,0},{2,15},{3,14},... | collective-permute-start | bytes 196616 | tf_op jit(solution)/shard_map/ppermute | solution.py:300
  13.0 3.7 %collective-permute-start.3 = (bf16[32,1024]{1,0:T(8,128)(2,1)S(1)}, bf16[32,1024]{1,0:T(8,128)(2,1)S(1)}, u32[]{:S(2)}, u32[]{:S(2)}) collective-permute-start(bf16[32,1024]{1,0:T(8,128)(2,1)S(1)} %shard_map.58), channel_id=1, source_target_pairs={{0,1},{1,0},{2,3},{3,2},{4,5},{5,4},{6,7},{7,6},{8,9},{9,8},{10,11... | collective-permute-start | bytes 196616 | tf_op jit(solution)/shard_map/ppermute | solution.py:304

commit v9 on v8

--- a/solution.py
+++ b/solution.py
@@ -11,7 +11,8 @@
 MAXOFF = 32
 SHIFT = 32
 LANES = 128
-FINE = 8
+FINE = 4
+SUBLANES = 8
 PLANES = (MAXOFF - 1 + FINE - 1) // FINE + 1
 
 
@@ -78,7 +79,7 @@
     rows = delay_row.shape[1]
     leaf_rows = columns + span
     lhs_rows = leaf_rows + FINE * (PLANES - 1)
-    time_rows = lhs_rows + FINE
+    time_rows = lhs_rows + SUBLANES
     turned = jnp.transpose(jnp.concatenate([window] * (LANES // band), axis=0)).astype(jnp.float32)
     time_ref[:time_rows, :] = turned[:time_rows, :]
     low_lanes = lax.broadcasted_iota(jnp.int32, (lhs_rows, LANES), 1) < band
@@ -219,14 +220,14 @@
     core_count = lax.axis_size("trial")
     rows = trials // core_count
     span = levels * SHIFT
-    tail = -(-(MAXOFF - 1 + span) // LANES) * LANES
+    tail = -(-(span + FINE * (PLANES - 1) + SUBLANES) // LANES) * LANES
     body = seg - tail
 
     def scratch(columns):
         leaf_rows = columns + span
         lhs_rows = leaf_rows + FINE * (PLANES - 1)
         return (
-            pltpu.VMEM((lhs_rows + FINE, LANES), jnp.float32),
+            pltpu.VMEM((lhs_rows + SUBLANES, LANES), jnp.float32),
             pltpu.VMEM((lhs_rows, FINE * band), jnp.bfloat16),
             pltpu.VMEM((lhs_rows, PLANES * rows), jnp.float32),
             pltpu.VMEM((leaf_rows, rows), jnp.float32),

time: 17.6 us -> 17.4 us (0.989)
  no operation moved by 1% of the time
where the time goes in v9:
time: 17.4 us; the launch traced here: 17.3 us
  starting transfers between devices  8.11 us (47%)
  waiting for transfers between devices  5.76 us (33%)
  Pallas kernels  3.35 us (19%)
    ppermute x2, starting transfers between devices, traded(): arrived.append(lax.ppermute(block, ('freq', 'trial'), route))  4.96 us
    pallas_call x5, Pallas kernels, call(): pl.pallas_call(kernel, out_shape=outs, **specs, scratch_shapes=list(scrat...  3.35 us
    ppermute x1, waiting for transfers between devices, shards(): far = lax.ppermute(far, ('freq', 'trial'), route)  3.32 us
    ppermute x1, waiting for transfers between devices, shards(): following = lax.ppermute(edge, ('tm', 'trial'), ring)  2.4 us
    ppermute x1, starting transfers between devices, shards(): far = lax.ppermute(far, ('freq', 'trial'), route)  1.75 us
    ppermute x1, starting transfers between devices, shards(): following = lax.ppermute(edge, ('tm', 'trial'), ring)  1.04 us
    ppermute x1, starting transfers between devices, shards(): received += [*both, lax.ppermute(handed, 'trial', [(0, 1), (1, 0)])]  0.37 us
  transfers between devices with their start and end apart: 5, of which 2 were waited for; matrix products, arithmetic and copies ran while one was open for 0% of the time, Pallas kernels for 3%

profile of v9, /device:TPU:1, one launch (start us, length us, event | category | flops | bytes accessed | tf_op | source)
XLA Modules:
  0.0 17.3 jit_solution(2582370525676123030)
XLA Ops:
  0.0 1.0 %shard_map.55 = (bf16[64,128]{1,0:T(8,128)(2,1)S(1)}, bf16[64,1024]{1,0:T(8,128)(2,1)S(1)}, s32[64,256]{1,0:T(8,128)S(1)}, bf16[64,256]{1,0:T(8,128)(2,1)S(1)}, s32[8,128]{1,0:T(8,128)S(1)}) custom-call(bf16[64,1024]{1,0:T(8,128)(2,1)} %x_hbm.1, s32[64,256]{1,0:T(8,128)} %bitcast.6, bf16[64,256]{1,0:T(8,128)(2,1)} %bitcast.7, s32[1,256]{1,0:T(1,128)} %map_hbm.1, ...), custom_call_target="tpu_custom_call" | custom-call | tf_op jit(solution)/shard_map/pallas_call | solution.py:201
  1.0 1.2 %shard_map.56 = (bf16[256,1152]{1,0:T(8,128)(2,1)S(1)}, bf16[32,896]{1,0:T(8,128)(2,1)S(1)}, bf16[64,896]{1,0:T(8,128)(2,1)S(1)}, bf16[32,896]{1,0:T(8,128)(2,1)S(1)}) custom-call(bf16[64,1024]{1,0:T(8,128)(2,1)S(1)} %get-tuple-element.17.x_ref, s32[64,256]{1,0:T(8,128)S(1)} %get-tuple-element.18.off_ref, bf16[64,256]{1,0:T(8,128)(2,1)S(1)} %get-tuple-element.19.wt_ref, ...), custom_call_target="tpu_custom_call" | custom-call | tf_op jit(solution)/shard_map/pallas_call | solution.py:201
  2.2 3.2 %collective-permute-start.1 = (bf16[64,896]{1,0:T(8,128)(2,1)S(1)}, bf16[64,896]{1,0:T(8,128)(2,1)S(1)}, u32[]{:S(2)}, u32[]{:S(2)}) collective-permute-start(bf16[64,896]{1,0:T(8,128)(2,1)S(1)} %get-tuple-element.26), channel_id=1, source_target_pairs={{0,4},{1,9},{4,0},{5,13},{8,12},{9,1},{12,8},{13,5},{2,6},{3,11},{... | collective-permute-start | bytes 344072 | tf_op jit(solution)/shard_map/ppermute | solution.py:284
  5.4 1.0 %collective-permute-start = (bf16[64,128]{1,0:T(8,128)(2,1)S(1)}, bf16[64,128]{1,0:T(8,128)(2,1)S(1)}, u32[]{:S(2)}, u32[]{:S(2)}) collective-permute-start(bf16[64,128]{1,0:T(8,128)(2,1)S(1)} %get-tuple-element.22), channel_id=1, source_target_pairs={{3,0},{2,1},{1,2},{0,3},{7,4},{6,5},{5,6},{4,7},{11,8},{10,9},{9,1... | collective-permute-start | bytes 49160 | tf_op jit(solution)/shard_map/ppermute | solution.py:262
  6.5 2.4 %collective-permute-done.next_ref = bf16[64,128]{1,0:T(8,128)(2,1)S(1)} collective-permute-done((bf16[64,128]{1,0:T(8,128)(2,1)S(1)}, bf16[64,128]{1,0:T(8,128)(2,1)S(1)}, u32[]{:S(2)}, u32[]{:S(2)}) %collective-permute-start) | collective-permute-done | bytes 16416 | tf_op jit(solution)/shard_map/ppermute | solution.py:262
  8.8 0.5 %shard_map.57 = (bf16[32,128]{1,0:T(8,128)(2,1)S(1)}, bf16[64,128]{1,0:T(8,128)(2,1)S(1)}, bf16[32,1024]{1,0:T(8,128)(2,1)S(1)}) custom-call(bf16[64,1024]{1,0:T(8,128)(2,1)S(1)} %get-tuple-element.17.x_ref, bf16[64,128]{1,0:T(8,128)(2,1)S(1)} %collective-permute-done.next_ref, bf16[256,1152]{1,0:T(8,128)(2,1)S(1)} %get-tuple-element.23.rhs_ref, ...), custom_call_target="tpu_custom_call" | custom-call | tf_op jit(solution)/shard_map/pallas_call | solution.py:201
  9.3 1.8 %collective-permute-start.2 = (bf16[64,128]{1,0:T(8,128)(2,1)S(1)}, bf16[64,128]{1,0:T(8,128)(2,1)S(1)}, u32[]{:S(2)}, u32[]{:S(2)}) collective-permute-start(bf16[64,128]{1,0:T(8,128)(2,1)S(1)} %get-tuple-element.27), channel_id=1, source_target_pairs={{0,4},{1,9},{4,0},{5,13},{8,12},{9,1},{12,8},{13,5},{2,6},{3,11},{... | collective-permute-start | bytes 49160 | tf_op jit(solution)/shard_map/ppermute | solution.py:284
  11.1 1.7 %collective-permute-start.4 = (bf16[32,1024]{1,0:T(8,128)(2,1)S(1)}, bf16[32,1024]{1,0:T(8,128)(2,1)S(1)}, u32[]{:S(2)}, u32[]{:S(2)}) collective-permute-start(bf16[32,1024]{1,0:T(8,128)(2,1)S(1)} %get-tuple-element.28), channel_id=1, source_target_pairs={{0,13},{1,12},{4,9},{5,8},{8,5},{9,4},{12,1},{13,0},{2,15},{3,14},... | collective-permute-start | bytes 196616 | tf_op jit(solution)/shard_map/ppermute | solution.py:301
  12.8 0.0 collective-permute-done.2.tail_ref.refs_3_
  12.9 0.0 collective-permute-done.1.body_ref.refs_2_
  12.9 0.4 %collective-permute-start.3 = (bf16[32,1024]{1,0:T(8,128)(2,1)S(1)}, bf16[32,1024]{1,0:T(8,128)(2,1)S(1)}, u32[]{:S(2)}, u32[]{:S(2)}) collective-permute-start(bf16[32,1024]{1,0:T(8,128)(2,1)S(1)} %shard_map.58), channel_id=1, source_target_pairs={{0,1},{1,0},{2,3},{3,2},{4,5},{5,4},{6,7},{7,6},{8,9},{9,8},{10,11... | collective-permute-start | bytes 196616 | tf_op jit(solution)/shard_map/ppermute | solution.py:305
  13.3 3.3 %collective-permute-done.4.refs_5_ = bf16[32,1024]{1,0:T(8,128)(2,1)S(1)} collective-permute-done((bf16[32,1024]{1,0:T(8,128)(2,1)S(1)}, bf16[32,1024]{1,0:T(8,128)(2,1)S(1)}, u32[]{:S(2)}, u32[]{:S(2)}) %collective-permute-start.4) | collective-permute-done | bytes 65568 | tf_op jit(solution)/shard_map/ppermute | solution.py:301
  16.6 0.0 collective-permute-done.3.refs_4_
  16.6 0.7 %shard_map.59 = bf16[32,1024]{1,0:T(8,128)(2,1)} custom-call(bf16[32,896]{1,0:T(8,128)(2,1)S(1)} %get-tuple-element.21.refs_0_, bf16[32,128]{1,0:T(8,128)(2,1)S(1)} %get-tuple-element.25.refs_1_, bf16[64,896]{1,0:T(8,128)(2,1)S(1)} %collective-permute-done.1.body_ref.refs_2_, bf16[64,128]{1,0:T(8,128)(2,1)S(1)} %collective-permute-done.2.tail_ref.refs_3_, ...), custom_call_target="tpu_custom_call" | custom-call | tf_op jit(solution)/shard_map/pallas_call | solution.py:201
  (1 shorter events, 0.0 us)
Async XLA Ops:
  2.2 10.7 %collective-permute-start.1 = (bf16[64,896]{1,0:T(8,128)(2,1)S(1)}, bf16[64,896]{1,0:T(8,128)(2,1)S(1)}, u32[]{:S(2)}, u32[]{:S(2)}) collective-permute-start(bf16[64,896]{1,0:T(8,128)(2,1)S(1)} %get-tuple-element.26), channel_id=1, source_target_pairs={{0,4},{1,9},{4,0},{5,13},{8,12},{9,1},{12,8},{13,5},{2,6},{3,11},{... | collective-permute-start | bytes 344072 | tf_op jit(solution)/shard_map/ppermute | solution.py:284
  5.4 3.4 %collective-permute-start = (bf16[64,128]{1,0:T(8,128)(2,1)S(1)}, bf16[64,128]{1,0:T(8,128)(2,1)S(1)}, u32[]{:S(2)}, u32[]{:S(2)}) collective-permute-start(bf16[64,128]{1,0:T(8,128)(2,1)S(1)} %get-tuple-element.22), channel_id=1, source_target_pairs={{3,0},{2,1},{1,2},{0,3},{7,4},{6,5},{5,6},{4,7},{11,8},{10,9},{9,1... | collective-permute-start | bytes 49160 | tf_op jit(solution)/shard_map/ppermute | solution.py:262
  9.3 3.6 %collective-permute-start.2 = (bf16[64,128]{1,0:T(8,128)(2,1)S(1)}, bf16[64,128]{1,0:T(8,128)(2,1)S(1)}, u32[]{:S(2)}, u32[]{:S(2)}) collective-permute-start(bf16[64,128]{1,0:T(8,128)(2,1)S(1)} %get-tuple-element.27), channel_id=1, source_target_pairs={{0,4},{1,9},{4,0},{5,13},{8,12},{9,1},{12,8},{13,5},{2,6},{3,11},{... | collective-permute-start | bytes 49160 | tf_op jit(solution)/shard_map/ppermute | solution.py:284
  11.1 5.5 %collective-permute-start.4 = (bf16[32,1024]{1,0:T(8,128)(2,1)S(1)}, bf16[32,1024]{1,0:T(8,128)(2,1)S(1)}, u32[]{:S(2)}, u32[]{:S(2)}) collective-permute-start(bf16[32,1024]{1,0:T(8,128)(2,1)S(1)} %get-tuple-element.28), channel_id=1, source_target_pairs={{0,13},{1,12},{4,9},{5,8},{8,5},{9,4},{12,1},{13,0},{2,15},{3,14},... | collective-permute-start | bytes 196616 | tf_op jit(solution)/shard_map/ppermute | solution.py:301
  12.9 3.7 %collective-permute-start.3 = (bf16[32,1024]{1,0:T(8,128)(2,1)S(1)}, bf16[32,1024]{1,0:T(8,128)(2,1)S(1)}, u32[]{:S(2)}, u32[]{:S(2)}) collective-permute-start(bf16[32,1024]{1,0:T(8,128)(2,1)S(1)} %shard_map.58), channel_id=1, source_target_pairs={{0,1},{1,0},{2,3},{3,2},{4,5},{5,4},{6,7},{7,6},{8,9},{9,8},{10,11... | collective-permute-start | bytes 196616 | tf_op jit(solution)/shard_map/ppermute | solution.py:305
